TPU v7x, 32 devices: a whole 2x2x4 slice. The times are simulated.
32 devices in a mesh: grp: 4 (over x, core), gx: 2 (over y), gy: 4 (over z).
Axes of the slice: x: 2, y: 2, z: 4, core: 2. Of those that a mesh axis runs over, the one named last changes fastest.
Arguments:
- sources: float32 [4, 8, 32, 512], P('grp', 'gx', 'gy'), may hold values from -4.5 to 5.5
- diagonal: float32 [8, 32, 512], P('gx', 'gy'), may hold values from 0.02 to 0.3
- coarse_ids: int32 [8, 32, 512], P('gx', 'gy'), may hold values from 0 to 255, as said below
- coarse_inverse: float32 [256, 256], replicated, may hold values from -1 to 3
- omega_rows: float32 [4, 32], replicated, may hold values from -5 to 5
- psi: float32 [32, 8, 32, 512], P(None, 'gx', 'gy', 'grp'), may hold values from -0.015625 to 0.015625
- phi: float32 [64, 8, 32, 512], P(None, 'gx', 'gy', 'grp'), may hold values from -0.015625 to 0.015625
- xi_cols: float32 [64, 4], replicated, may hold values from -5 to 5
- range_sketch: float32 [32, 8, 32, 512], P(None, 'gx', 'gy', 'grp'), may hold values from -3 to 3
- core_sketch: float32 [64, 64], replicated, may hold values from -2 to 2
Outputs:
- range_new: float32 [32, 8, 32, 512], P(None, 'gx', 'gy', 'grp')
- corange_cols: float32 [32, 4], replicated
- core_new: float32 [64, 64], replicated
Inputs may be any that keep to these rules, and one draw needn't show every extreme that they name: `coarse_ids`: the grid is cut into 4, 4 and 16 non-empty ranges of consecutive cells along the three dimensions; coarse cell (a * 4 + b) * 16 + c is the box of ranges a, b, c.
All inputs are finite; a program needn't handle non-finite values.
Results may differ from a plain program's by a relative error of at most 0.0003.
Values sent between devices are 32-bit elements; how exact they have to be, the bound alone decides.
No kernel may reach another device: no remote copies, remote signals or barrier semaphores. Data moves between devices by JAX's collectives and lax.ppermute only.
A program may use at most 64 MiB of HBM per device.

v0:
```python
import functools

import jax
import jax.numpy as jnp
from jax import lax
from jax.experimental import pallas as pl
from jax.experimental.pallas import tpu as pltpu
from jax.sharding import PartitionSpec as P


OUTER = 2
SWEEPS = 4
XY_CUTS = 4
Z_CUTS = 16
XY_BITS = XY_CUTS.bit_length() - 1
Z_BITS = Z_CUTS.bit_length() - 1
LANES = 128
SUBLANES = 8
VMEM_BYTES = 16 * 2**20

jacobi_weight = 2.0 / 3.0
highest = lax.Precision.HIGHEST


def dot_nt(a, b):
    return lax.dot_general(
        a, b, (((1,), (1,)), ((), ())), precision=highest, preferred_element_type=jnp.float32
    )


def dot_tn(a, b):
    return lax.dot_general(
        a, b, (((0,), (0,)), ((), ())), precision=highest, preferred_element_type=jnp.float32
    )


def iota(shape, dim):
    return lax.broadcasted_iota(jnp.int32, shape, dim)


def store_copies(out_ref, rows):
    for copy in range(out_ref.shape[0]):
        for at, row in enumerate(rows):
            out_ref[copy, at : at + 1, :] = row


def box_of(ids_ref, at):
    return lax.shift_right_logical(ids_ref[at, :, :LANES], Z_BITS)


def restrict(values, ids_ref, planes, coarse):
    cells_z = values.shape[1]
    rows_y = ids_ref.shape[1]
    ranks = lax.bitwise_and(ids_ref[0, 0:1, :], Z_CUTS - 1)
    members = lax.bitwise_and(iota((LANES, cells_z), 0), Z_CUTS - 1) == ranks
    sums = dot_nt(values, members.astype(jnp.float32))
    lane_box = lax.shift_right_logical(iota((rows_y, LANES), 1), Z_BITS)
    rows = []
    for part in range(coarse // LANES):
        total = None
        for at, plane in enumerate(planes):
            own = box_of(ids_ref, plane) == lane_box + part * (LANES // Z_CUTS)
            kept = jnp.where(own, sums[at * rows_y : (at + 1) * rows_y], 0.0)
            total = kept if total is None else total + kept
        rows.append(jnp.sum(total, axis=0, keepdims=True))
    return rows


def begin_kernel(
    source_from, diagonal_from, ids_from, inverse_from,
    mine_ref, ids_ref, inverse_ref, out_ref, arrived,
):
    loads = [
        pltpu.make_async_copy(source, target, arrived.at[at])
        for at, (source, target) in enumerate(
            (
                (ids_from, ids_ref),
                (source_from, mine_ref.at[0]),
                (diagonal_from, mine_ref.at[1]),
                (inverse_from, inverse_ref),
            )
        )
    ]
    for load in loads:
        load.start()
    coarse = inverse_ref.shape[0]
    rows_x, rows_y, cells_z = ids_ref.shape
    loads[0].wait()
    lanes = iota((1, LANES), 1)
    boxes = [box_of(ids_ref, at) for at in range(rows_x)]
    below_x = jnp.zeros((1, LANES), jnp.float32)
    for box in boxes:
        below_x = below_x + (lax.shift_right_logical(box[0:1], XY_BITS) <= lanes).astype(jnp.float32)
    ranks_y = lax.bitwise_and(boxes[0], XY_CUTS - 1)
    below_y = jnp.sum((ranks_y <= lanes - XY_CUTS).astype(jnp.float32), axis=0, keepdims=True)
    loads[1].wait()
    rows = restrict(
        mine_ref[0].reshape(rows_x * rows_y, cells_z), ids_ref, range(rows_x), coarse
    ) + [jnp.where(lanes < XY_CUTS, below_x, below_y)]
    for at, part in enumerate(rows):
        out_ref[at : at + 1, :] = part
    loads[2].wait()
    loads[3].wait()


def coarse_planes(rows, inverse_ref, ids_ref, scale_factor, cut_y, place):
    coarse = inverse_ref.shape[0]
    cells_z = ids_ref.shape[2]
    per_part = LANES // Z_CUTS
    row = jnp.broadcast_to(jnp.concatenate(rows, axis=1) * scale_factor, (SUBLANES, coarse))
    solved = dot_nt(row, inverse_ref[...])
    shape = (per_part, LANES)
    own = lax.shift_right_logical(iota(shape, 1), Z_BITS) == iota(shape, 0)
    lines = []
    for part in range(coarse // LANES):
        values = jnp.where(own, solved[:per_part, part * LANES : (part + 1) * LANES], 0.0)
        shift = LANES // 2
        while shift >= Z_CUTS:
            values = values + pltpu.roll(values, shift, 1)
            shift //= 2
        along_z = jnp.concatenate(
            [
                jnp.take_along_axis(
                    values,
                    lax.bitwise_and(ids_ref[0, :per_part, at : at + LANES], Z_CUTS - 1),
                    axis=1,
                )
                for at in range(0, cells_z, LANES)
            ],
            axis=1,
        )
        lines.extend(along_z[at : at + 1] for at in range(per_part))
    place_y, inside = place
    planes = []
    for box_x in range(XY_CUTS):
        first = box_x * XY_CUTS
        plane = jnp.broadcast_to(lines[first], place_y.shape)
        for box_y in range(1, XY_CUTS):
            plane = jnp.where(place_y >= cut_y[box_y - 1], lines[first + box_y], plane)
        planes.append(jnp.where(inside, plane, 0.0))
    return planes


def correction_of(planes, cut_x, place_x):
    value = planes[0]
    for box_x in range(1, XY_CUTS):
        value = jnp.where(cut_x[box_x - 1] <= place_x, planes[box_x], value)
    return value


def cuts_of(row, count_x, count_y):
    cut_x = [row[:, at : at + 1] * (1.0 / count_y) for at in range(XY_CUTS - 1)]
    cut_y = [row[:, XY_CUTS + at : XY_CUTS + at + 1] * (1.0 / count_x) for at in range(XY_CUTS - 1)]
    return cut_x, cut_y


def beside_z(values):
    lanes = iota((values.shape[0], LANES), 1)
    tiles = [values[:, at : at + LANES] for at in range(0, values.shape[1], LANES)]
    empty = jnp.zeros_like(tiles[0])
    ahead = [pltpu.roll(tile, LANES - 1, 1) for tile in tiles] + [empty]
    behind = [empty] + [pltpu.roll(tile, 1, 1) for tile in tiles]
    return jnp.concatenate(
        [
            jnp.where(lanes == LANES - 1, ahead[at + 1], ahead[at])
            + jnp.where(lanes == 0, behind[at], behind[at + 1])
            for at in range(len(tiles))
        ],
        axis=1,
    )


def beside_y(values):
    rows = values.shape[0]
    return pltpu.roll(values, rows - 1, 0) + pltpu.roll(values, 1, 0)


def neighbours(field_ref, at, rows=None):
    center = field_ref[at + 1]
    along_y = beside_y(center)
    if rows is None:
        rows = slice(0, center.shape[0])
    center = center[rows]
    across = field_ref[at, rows, :] + field_ref[at + 2, rows, :]
    return center, across + along_y[rows] + beside_z(center)


def smooth(field_ref, weight_ref, drive_ref, at, rows=None):
    center, beside = neighbours(field_ref, at, rows)
    rows = slice(None) if rows is None else rows
    kept = center * (1.0 - jacobi_weight) + drive_ref[at, rows, :]
    return kept + weight_ref[at, rows, :] * beside


def sweep(from_ref, to_ref, weight_ref, drive_ref, rows_x, reach):
    window_x, window_y, _ = weight_ref.shape
    own_rows = slice(window_y // 3, 2 * window_y // 3)
    for at in range(window_x):
        away = max(0, at - rows_x + 1)
        if away > reach:
            continue
        if away == reach:
            to_ref[at + 1, own_rows, :] = smooth(from_ref, weight_ref, drive_ref, at, own_rows)
        else:
            to_ref[at + 1] = smooth(from_ref, weight_ref, drive_ref, at)


def window_place(count_y, rows_y, shape):
    place_y = iota(shape, 0) + (lax.axis_index("gy") - 1) * rows_y
    inside = (place_y >= 0) & (place_y < rows_y * count_y)
    return place_y.astype(jnp.float32), inside


def mirrored(at, last):
    return jnp.where(lax.axis_index("gx") == 0, at, last - at)


def add_correction(planes, cut_x, window_x, planes_used, from_ref, to_ref):
    for at in range(planes_used):
        place_x = mirrored(at, window_x - 1).astype(jnp.float32)
        value = correction_of(planes, cut_x, place_x)
        to_ref[at + 1] = value if from_ref is None else from_ref[at + 1] + value


def clear_ends(field_ref, window_x):
    empty = jnp.zeros(field_ref.shape[1:], jnp.float32)
    field_ref[0] = empty
    field_ref[window_x + 1] = empty


def first_kernel(
    counts, scale_factor, own_ref, other_ref, even_ref, even_other_ref, odd_ref, odd_other_ref,
    ids_ref, inverse_ref, gathered_ref,
    field_ref, weight_ref, drive_ref, out_ref, spare_ref,
):
    count_x, count_y = counts
    _, rows_x, rows_y, cells_z = own_ref.shape
    window_x, window_y, _ = weight_ref.shape
    at_y = lax.axis_index("gy")
    parity = lax.rem(at_y, 2)
    even_row = pl.multiple_of((1 - parity) * 2 * rows_y, SUBLANES)
    odd_row = pl.multiple_of(parity * 2 * rows_y, SUBLANES)
    odd_inside = jnp.where((at_y > 0) & (at_y < count_y - 1), jacobi_weight, 0.0)
    for ref, first, row, scale in (
        (own_ref, 0, rows_y, jacobi_weight),
        (other_ref, rows_x, rows_y, jacobi_weight),
        (even_ref, 0, even_row, jacobi_weight),
        (even_other_ref, rows_x, even_row, jacobi_weight),
        (odd_ref, 0, odd_row, odd_inside),
        (odd_other_ref, rows_x, odd_row, odd_inside),
    ):
        for at in range(rows_x):
            plane = mirrored(at, rows_x - 1)
            weight = scale / (6.0 + ref[1, plane])
            weight_ref[first + at, pl.ds(row, rows_y), :] = weight
            drive_ref[first + at, pl.ds(row, rows_y), :] = weight * ref[0, plane]

    parts = inverse_ref.shape[0] // LANES
    rows = [gathered_ref[at : at + 1] for at in range(parts + 1)]
    cut_x, cut_y = cuts_of(rows[parts], count_x, count_y)
    place = window_place(count_y, rows_y, (window_y, cells_z))
    planes = coarse_planes(rows[:parts], inverse_ref, ids_ref, scale_factor, cut_y, place)
    clear_ends(field_ref, window_x)
    clear_ends(spare_ref, window_x)
    add_correction(planes, cut_x, window_x, window_x, None, field_ref)
    for step in range(SWEEPS):
        refs = (field_ref, spare_ref) if step % 2 == 0 else (spare_ref, field_ref)
        sweep(*refs, weight_ref, drive_ref, rows_x, 2 * SWEEPS - 1 - step)

    residual, used = [], []
    own_rows = slice(rows_y, 2 * rows_y)
    for at in range(rows_x):
        plane = mirrored(at, rows_x - 1)
        center, beside = neighbours(field_ref, at, own_rows)
        residual.append(own_ref[0, plane] - ((6.0 + own_ref[1, plane]) * center - beside))
        used.append(plane)
    partial = restrict(jnp.concatenate(residual, axis=0), ids_ref, used, inverse_ref.shape[0])
    store_copies(out_ref, partial + rows[parts:])


def second_kernel(
    counts, scale_factor, pieces,
    field_ref, weight_ref, drive_ref, ids_ref, inverse_ref, gathered_ref, *rest,
):
    out_refs, (one_ref, two_ref) = rest[:pieces], rest[pieces:]
    count_x, count_y = counts
    window_x, window_y, cells_z = weight_ref.shape
    rows_x, rows_y, chunk = out_refs[0].shape
    parts = inverse_ref.shape[0] // LANES
    gathered = jnp.sum(gathered_ref[...], axis=0)
    rows = [gathered[at : at + 1] for at in range(parts)]
    cut_x, cut_y = cuts_of(gathered_ref[0, parts : parts + 1], count_x, count_y)
    place = window_place(count_y, rows_y, (window_y, cells_z))
    planes = coarse_planes(rows, inverse_ref, ids_ref, scale_factor, cut_y, place)
    clear_ends(one_ref, window_x)
    clear_ends(two_ref, window_x)
    used = min(window_x, rows_x + SWEEPS)
    add_correction(planes, cut_x, window_x, used, field_ref, one_ref)
    fields = [one_ref, two_ref]
    for step in range(SWEEPS - 1):
        sweep(*fields, weight_ref, drive_ref, rows_x, SWEEPS - 1 - step)
        fields.reverse()
    last_ref, own_ref = fields
    own_rows = slice(rows_y, 2 * rows_y)
    for at in range(rows_x):
        value = smooth(last_ref, weight_ref, drive_ref, at, own_rows)
        own_ref[mirrored(at, rows_x - 1), pl.ds(0, rows_y), :] = value
    me = lax.axis_index("grp")
    for turn in range(pieces):
        first = pl.multiple_of(lax.bitwise_xor(me, turn) * chunk, LANES)
        for at in range(rows_x):
            out_refs[turn][at] = own_ref[at, pl.ds(0, rows_y), pl.ds(first, chunk)]


def range_kernel(pieces, omega_ref, range_ref, *rest):
    snaps, (new_ref,) = rest[:pieces], rest[pieces:]
    rows_x = range_ref.shape[1]
    me = lax.axis_index("grp")
    slots = [lax.bitwise_xor(me, turn) for turn in range(pieces)]
    cells = [[snaps[turn][at] for at in range(rows_x)] for turn in range(pieces)]
    for at_row in range(range_ref.shape[0]):
        scales = [omega_ref[slots[turn], at_row] for turn in range(pieces)]
        for at in range(rows_x):
            value = range_ref[at_row, at]
            for turn in range(pieces):
                value = value + scales[turn] * cells[turn][at]
            new_ref[at_row, at] = value


def sum_rows(values):
    sublanes = iota(values[0].shape, 0)
    shift = SUBLANES // 2
    while shift:
        low = lax.bitwise_and(sublanes, shift) == 0
        half = len(values) // 2
        values = [
            jnp.where(
                low,
                values[at] + pltpu.roll(values[at], SUBLANES - shift, 0),
                values[at + half] + pltpu.roll(values[at + half], shift, 0),
            )
            for at in range(half)
        ]
        shift //= 2
    return values[0]


def products(psi_ref, phi_ref, snaps):
    rows_x = psi_ref.shape[1]
    cells = [[snap[at] for at in range(rows_x)] for snap in snaps]
    kept = [[] for _ in snaps]
    for ref in (psi_ref, phi_ref):
        for first in range(0, ref.shape[0], SUBLANES):
            totals = [[] for _ in snaps]
            for at_row in range(first, first + SUBLANES):
                parts = [ref[at_row, at] for at in range(rows_x)]
                for turn in range(len(snaps)):
                    total = parts[0] * cells[turn][0]
                    for at in range(1, rows_x):
                        total = total + parts[at] * cells[turn][at]
                    totals[turn].append(total)
            for turn in range(len(snaps)):
                kept[turn].append(sum_rows(totals[turn]))
    count = psi_ref.shape[0] + phi_ref.shape[0]
    rest = [jnp.zeros((LANES - count, LANES), jnp.float32)] if count < LANES else []
    ones = jnp.ones((SUBLANES, LANES), jnp.float32)
    return [dot_nt(ones, jnp.concatenate(rows + rest, axis=0))[0:1] for rows in kept]


def early_kernel(pieces, psi_ref, phi_ref, *rest):
    snaps, (out_ref,) = rest[:pieces], rest[pieces:]
    for at, row in enumerate(products(psi_ref, phi_ref, snaps)):
        out_ref[at : at + 1, :] = row


def late_kernel(pieces, psi_ref, phi_ref, early_ref, *rest):
    snaps, (out_ref,) = rest[:pieces], rest[pieces:]
    me = lax.axis_index("grp")
    early = early_ref.shape[0]
    rows = [early_ref[at : at + 1, :] for at in range(early)]
    rows += products(psi_ref, phi_ref, snaps)
    for turn, row in enumerate(rows):
        slot = lax.bitwise_xor(me, turn)
        for copy in range(out_ref.shape[0]):
            out_ref[copy, pl.ds(slot, 1), :] = row


def end_kernel(gathered_ref, xi_ref, core_ref, corange_out_ref, core_out_ref):
    corange = corange_out_ref.shape[1]
    core = core_ref.shape[0]
    total = jnp.sum(gathered_ref[...], axis=0)
    corange_out_ref[...] = total[:, :corange]
    images = total[:, corange : corange + core]
    core_out_ref[...] = core_ref[...] + dot_tn(images, xi_ref[...])


vmem = pl.BlockSpec(memory_space=pltpu.VMEM)
smem = pl.BlockSpec(memory_space=pltpu.SMEM)


def call(kernel, outs, inputs, scratch=(), specs=None):
    many = isinstance(outs, list)
    shapes = [jax.ShapeDtypeStruct(shape, jnp.float32) for shape in (outs if many else [outs])]
    result = pl.pallas_call(
        kernel,
        out_shape=shapes,
        in_specs=specs or [vmem] * len(inputs),
        out_specs=[vmem] * len(shapes),
        scratch_shapes=[pltpu.VMEM(shape, jnp.float32) for shape in scratch],
        compiler_params=pltpu.CompilerParams(vmem_limit_bytes=VMEM_BYTES),
    )(*inputs)
    return result if many else result[0]


def in_hbm(array):
    return pltpu.with_memory_space_constraint(array, pltpu.HBM)


def gather(copies, axes):
    return lax.all_to_all(copies, axes, 0, 0)


def fast_body(
    sources, diagonal, coarse_ids, coarse_inverse, omega_rows, psi, phi, xi_cols, range_sketch,
    core_sketch,
):
    source = sources[0]
    rows_x, rows_y, cells_z = source.shape
    counts = (lax.axis_size("gx"), lax.axis_size("gy"))
    groups = lax.axis_size("grp")
    count_x, count_y = counts
    coarse = coarse_inverse.shape[0]
    scale_factor = coarse / (rows_x * count_x * rows_y * count_y * cells_z)
    window = (rows_x * count_x, 3 * rows_y, cells_z)
    padded = (window[0] + 2,) + window[1:]
    copies = (count_x * count_y, coarse // LANES + 1, LANES)

    def partner_y(at, phase):
        found = at ^ 1 if phase == 0 else ((at + 1) ^ 1) - 1
        return found if 0 <= found < count_y else at

    def pairs(cross, phase):
        return [
            (x * count_y + y, (x ^ cross) * count_y + (y if phase is None else partner_y(y, phase)))
            for x in range(count_x)
            for y in range(count_y)
        ]

    mine, ids, inverse, begin = pl.pallas_call(
        begin_kernel,
        out_shape=[
            jax.ShapeDtypeStruct((2,) + source.shape, jnp.float32),
            jax.ShapeDtypeStruct(coarse_ids.shape, jnp.int32),
            jax.ShapeDtypeStruct(coarse_inverse.shape, jnp.float32),
            jax.ShapeDtypeStruct(copies[1:], jnp.float32),
        ],
        in_specs=[pl.BlockSpec(memory_space=pltpu.HBM)] * 4,
        out_specs=[vmem] * 4,
        scratch_shapes=[pltpu.SemaphoreType.DMA((4,))],
        compiler_params=pltpu.CompilerParams(vmem_limit_bytes=VMEM_BYTES),
        name="begin",
    )(*map(in_hbm, (source, diagonal, coarse_ids, coarse_inverse)))
    others = []
    for at, (cross, phase) in enumerate(((1, None), (0, 0), (0, 0), (0, 1), (0, 1))):
        sent = others[0] if at in (2, 4) else mine
        others.append(lax.ppermute(sent, ("gx", "gy"), pairs(cross, phase)))
    gathered = begin
    bits = [1 << bit for bit in reversed(range(count_y.bit_length() - 1))]
    turns = [("gy", count_y, bit) for bit in bits]
    turns.insert(1, ("gx", count_x, 1))
    for axis, count, bit in turns:
        gathered = gathered + lax.ppermute(gathered, axis, [(i, i ^ bit) for i in range(count)])
    field, weight, drive, partial = call(
        functools.partial(first_kernel, counts, scale_factor),
        [padded, window, window, copies],
        (mine, *others, ids, inverse, gathered),
        scratch=[padded],
    )
    gathered = gather(partial, ("gx", "gy"))
    chunk = cells_z // groups
    pieces = call(
        functools.partial(second_kernel, counts, scale_factor, groups),
        [(rows_x, rows_y, chunk)] * groups,
        (field, weight, drive, ids, inverse, gathered),
        scratch=[padded, padded],
    )
    snaps = [pieces[0]] + [
        lax.ppermute(pieces[turn], "grp", [(at, at ^ turn) for at in range(groups)])
        for turn in range(1, groups)
    ]
    early = max(1, groups // 2)
    kept = call(functools.partial(early_kernel, early), (early, LANES), (psi, phi, *snaps[:early]))
    sketched = call(
        functools.partial(late_kernel, groups - early),
        (groups * count_x * count_y, groups, LANES),
        (psi, phi, kept, *snaps[early:]),
    )
    gathered = gather(sketched, ("grp", "gx", "gy"))
    range_new = call(
        functools.partial(range_kernel, groups),
        range_sketch.shape,
        (omega_rows, range_sketch, *snaps),
        specs=[smem] + [vmem] * (1 + groups),
    )
    corange_cols, core_new = call(
        end_kernel, [(groups, psi.shape[0]), core_sketch.shape], (gathered, xi_cols.T, core_sketch)
    )
    return range_new, corange_cols.T, core_new


def with_halo(cells, sides, width):
    for axis, dim in sides:
        count = lax.axis_size(axis)
        ends = count - 1
        head = lax.slice_in_dim(cells, 0, width, axis=dim)
        tail = lax.slice_in_dim(cells, cells.shape[dim] - width, cells.shape[dim], axis=dim)
        cells = jnp.concatenate(
            [
                lax.ppermute(tail, axis, [(i, (i + 1) % count) for i in range(ends)]),
                cells,
                lax.ppermute(head, axis, [((i + 1) % count, i) for i in range(ends)]),
            ],
            axis=dim,
        )
    return cells


def neighbour_image(widened, diagonal):
    center = widened[1:-1, 1:-1]
    beside = widened[2:, 1:-1] + widened[:-2, 1:-1]
    beside = beside + widened[1:-1, 2:] + widened[1:-1, :-2]
    padded = jnp.pad(center, ((0, 0), (0, 0), (1, 1)))
    beside = beside + padded[:, :, 2:] + padded[:, :, :-2]
    return (center, (6.0 + diagonal) * center - beside)


def smooth_once(widened, source, diagonal):
    center, applied = neighbour_image(widened, diagonal)
    return center + jacobi_weight * (source - applied) / (6.0 + diagonal)


def axis_maps(coarse_ids):
    ranks_x = coarse_ids[:, 0, 0] // (XY_CUTS * Z_CUTS)
    ranks_y = coarse_ids[0, :, 0] // Z_CUTS % XY_CUTS
    ranks_z = coarse_ids[0, 0, :] % Z_CUTS
    cuts_xy = jnp.arange(XY_CUTS, dtype=jnp.int32)
    cuts_z = jnp.arange(Z_CUTS, dtype=jnp.int32)
    map_x = (ranks_x[:, None] == cuts_xy[None, :]).astype(jnp.float32)
    map_y = (ranks_y[:, None] == cuts_xy[None, :]).astype(jnp.float32)
    map_z = (ranks_z[:, None] == cuts_z[None, :]).astype(jnp.float32)
    return (map_x, map_y, map_z)


def restrict_cells(values, maps):
    map_x, map_y, map_z = maps
    rows_x, rows_y, cells_z = values.shape
    along_z = jnp.dot(values.reshape(rows_x * rows_y, cells_z), map_z, precision=highest)
    along_z = along_z.reshape(rows_x, rows_y, Z_CUTS)
    along_y = jnp.einsum("xyc,yb->xbc", along_z, map_y, precision=highest)
    along_x = jnp.einsum("xbc,xa->abc", along_y, map_x, precision=highest)
    return along_x.reshape(-1)


def prolong(correction, maps, extent):
    map_x, map_y, map_z = maps
    boxes = correction.reshape(XY_CUTS, XY_CUTS, Z_CUTS)
    over_x = jnp.einsum("abc,xa->xbc", boxes, map_x, precision=highest)
    over_y = jnp.einsum("xbc,yb->xyc", over_x, map_y, precision=highest)
    spread = jnp.dot(over_y.reshape(extent[0] * extent[1], Z_CUTS), map_z.T, precision=highest)
    return spread.reshape(extent)


def general_body(
    sources, diagonal, coarse_ids, coarse_inverse, omega_rows, psi, phi, xi_cols, range_sketch,
    core_sketch,
):
    source = sources[0]
    rows_x, rows_y, cells_z = source.shape
    coarse = coarse_inverse.shape[0]
    total_cells = rows_x * lax.axis_size("gx") * rows_y * lax.axis_size("gy") * cells_z
    scale_factor = coarse / total_cells
    maps = axis_maps(coarse_ids)
    sides = (("gx", 0), ("gy", 1))
    pressure = jnp.zeros_like(source)
    for outer_step in range(OUTER):
        if outer_step == 0:
            residual = source
        else:
            residual = source - neighbour_image(with_halo(pressure, sides, 1), diagonal)[1]
        coarse_rhs = lax.psum(restrict_cells(residual, maps), ("gx", "gy"))
        correction = jnp.dot(coarse_inverse, coarse_rhs * scale_factor, precision=highest)
        pressure = pressure + prolong(correction, maps, source.shape)
        for _ in range(SWEEPS):
            pressure = smooth_once(with_halo(pressure, sides, 1), source, diagonal)
    snapshot = lax.all_to_all(pressure[None], "grp", split_axis=3, concat_axis=0, tiled=True)
    columns = snapshot.reshape(snapshot.shape[0], -1)
    range_flat = range_sketch.reshape(range_sketch.shape[0], -1)
    range_new = range_flat + jnp.einsum("tk,tc->kc", omega_rows, columns, precision=highest)
    corange_part = jnp.einsum(
        "lc,tc->lt", psi.reshape(psi.shape[0], -1), columns, precision=highest
    )
    core_part = jnp.einsum("sc,tc->st", phi.reshape(phi.shape[0], -1), columns, precision=highest)
    corange_cols, core_images = lax.psum((corange_part, core_part), ("grp", "gx", "gy"))
    core_new = core_sketch + jnp.dot(core_images, xi_cols.T, precision=highest)
    return (range_new.reshape(range_sketch.shape), corange_cols, core_new)


def body(*arrays):
    _, rows_y, cells_z = arrays[1].shape
    coarse, groups = arrays[3].shape[0], lax.axis_size("grp")
    fits = (
        lax.axis_size("gx") == 2
        and lax.axis_size("gy") & (lax.axis_size("gy") - 1) == 0
        and lax.axis_size("gy") > 1
        and rows_y >= OUTER * SWEEPS
        and OUTER == 2
        and rows_y == SUBLANES
        and coarse == XY_CUTS * XY_CUTS * Z_CUTS
        and groups & (groups - 1) == 0
        and 1 < groups <= SUBLANES
        and cells_z % (groups * LANES) == 0
        and cells_z // groups == LANES
        and coarse % LANES == 0
        and arrays[5].shape[0] % SUBLANES == 0
        and arrays[6].shape[0] % SUBLANES == 0
        and arrays[5].shape[0] + arrays[6].shape[0] <= LANES
    )
    if not fits:
        return general_body(*arrays)
    return fast_body(*arrays)


def solution(mesh):
    return jax.shard_map(
        body,
        mesh=mesh,
        in_specs=(
            P("grp", "gx", "gy", None),
            P("gx", "gy", None),
            P("gx", "gy", None),
            P(),
            P(),
            P(None, "gx", "gy", "grp"),
            P(None, "gx", "gy", "grp"),
            P(),
            P(None, "gx", "gy", "grp"),
            P(),
        ),
        out_specs=(P(None, "gx", "gy", "grp"), P(), P()),
        check_vma=False,
    )
```

profile of v0, /device:TPU:0, one launch (start us, length us, event | category | flops | bytes accessed | tf_op | source)
XLA Modules:
  0.0 56.1 jit_solution(14646177733076427315)
XLA Ops:
  0.6 1.3 %begin.1 = (f32[2,4,8,512]{3,2,1,0:T(8,128)S(1)}, s32[4,8,512]{2,1,0:T(8,128)S(1)}, f32[256,256]{1,0:T(8,128)S(1)}, f32[3,128]{1,0:T(4,128)S(1)}) custom-call(f32[4,8,512]{2,1,0:T(8,128)} %bitcast.4, f32[4,8,512]{2,1,0:T(8,128)} %diagonal_from.1, s32[4,8,512]{2,1,0:T(8,128)} %ids_from.1, f32[256,256]{1,0:T(8,128)} %inverse_from.1), custom_call_target="tpu_custom_call" | custom-call | tf_op jit(solution)/shard_map/begin/pallas_call | solution.py:449
  1.9 3.1 %collective-permute-start = (f32[2,4,8,512]{3,2,1,0:T(8,128)S(1)}, f32[2,4,8,512]{3,2,1,0:T(8,128)S(1)}, u32[]{:S(2)}, u32[]{:S(2)}) collective-permute-start(f32[2,4,8,512]{3,2,1,0:T(8,128)S(1)} %get-tuple-element.17.own_ref), channel_id=1, source_target_pairs={{0,4},{1,5},{2,6},{3,7},{4,0},{5,1},{6,2},{7,3},{8,12},{9,13},{10,... | collective-permute-start | bytes 393224 | tf_op jit(solution)/shard_map/ppermute | solution.py:466
  5.0 0.7 %collective-permute-start.3 = (f32[2,4,8,512]{3,2,1,0:T(8,128)S(1)}, f32[2,4,8,512]{3,2,1,0:T(8,128)S(1)}, u32[]{:S(2)}, u32[]{:S(2)}) collective-permute-start(f32[2,4,8,512]{3,2,1,0:T(8,128)S(1)} %get-tuple-element.17.own_ref), channel_id=1, source_target_pairs={{0,0},{1,2},{2,1},{3,3},{4,4},{5,6},{6,5},{7,7},{8,8},{9,10},{10,9... | collective-permute-start | bytes 393224 | tf_op jit(solution)/shard_map/ppermute | solution.py:466
  5.7 4.5 %collective-permute-start.1 = (f32[2,4,8,512]{3,2,1,0:T(8,128)S(1)}, f32[2,4,8,512]{3,2,1,0:T(8,128)S(1)}, u32[]{:S(2)}, u32[]{:S(2)}) collective-permute-start(f32[2,4,8,512]{3,2,1,0:T(8,128)S(1)} %get-tuple-element.17.own_ref), channel_id=1, source_target_pairs={{0,1},{1,0},{2,3},{3,2},{4,5},{5,4},{6,7},{7,6},{8,9},{9,8},{10,11... | collective-permute-start | bytes 393224 | tf_op jit(solution)/shard_map/ppermute | solution.py:466
  10.1 0.0 collective-permute-done.other_ref
  10.1 0.7 %collective-permute-start.4 = (f32[2,4,8,512]{3,2,1,0:T(8,128)S(1)}, f32[2,4,8,512]{3,2,1,0:T(8,128)S(1)}, u32[]{:S(2)}, u32[]{:S(2)}) collective-permute-start(f32[2,4,8,512]{3,2,1,0:T(8,128)S(1)} %collective-permute-done.other_ref), channel_id=1, source_target_pairs={{0,0},{1,2},{2,1},{3,3},{4,4},{5,6},{6,5},{7,7},{8,8},{9,10},{10,9... | collective-permute-start | bytes 393224 | tf_op jit(solution)/shard_map/ppermute | solution.py:466
  10.8 3.0 %collective-permute-start.2 = (f32[2,4,8,512]{3,2,1,0:T(8,128)S(1)}, f32[2,4,8,512]{3,2,1,0:T(8,128)S(1)}, u32[]{:S(2)}, u32[]{:S(2)}) collective-permute-start(f32[2,4,8,512]{3,2,1,0:T(8,128)S(1)} %collective-permute-done.other_ref), channel_id=1, source_target_pairs={{0,1},{1,0},{2,3},{3,2},{4,5},{5,4},{6,7},{7,6},{8,9},{9,8},{10,11... | collective-permute-start | bytes 393224 | tf_op jit(solution)/shard_map/ppermute | solution.py:466
  13.8 0.0 collective-permute-start.5
  13.8 4.5 %collective-permute-done.5 = f32[3,128]{1,0:T(4,128)S(1)} collective-permute-done((f32[3,128]{1,0:T(4,128)S(1)}, f32[3,128]{1,0:T(4,128)S(1)}, u32[]{:S(2)}, u32[]{:S(2)}) %collective-permute-start.5) | collective-permute-done | bytes 1568 | tf_op jit(solution)/shard_map/ppermute | solution.py:472
  18.3 1.5 %collective-permute-start.6 = (f32[3,128]{1,0:T(4,128)S(1)}, f32[3,128]{1,0:T(4,128)S(1)}, u32[]{:S(2)}, u32[]{:S(2)}) collective-permute-start(f32[3,128]{1,0:T(4,128)S(1)} %add.9), channel_id=1, source_target_pairs={{0,4},{4,0},{1,5},{5,1},{2,6},{6,2},{3,7},{7,3},{8,12},{12,8},{9,1... | collective-permute-start | bytes 4616 | tf_op jit(solution)/shard_map/ppermute | solution.py:472
  19.8 2.1 %collective-permute-done.6 = f32[3,128]{1,0:T(4,128)S(1)} collective-permute-done((f32[3,128]{1,0:T(4,128)S(1)}, f32[3,128]{1,0:T(4,128)S(1)}, u32[]{:S(2)}, u32[]{:S(2)}) %collective-permute-start.6) | collective-permute-done | bytes 1568 | tf_op jit(solution)/shard_map/ppermute | solution.py:472
  21.9 0.4 collective-permute-start.7
  22.3 3.2 %collective-permute-done.7 = f32[3,128]{1,0:T(4,128)S(1)} collective-permute-done((f32[3,128]{1,0:T(4,128)S(1)}, f32[3,128]{1,0:T(4,128)S(1)}, u32[]{:S(2)}, u32[]{:S(2)}) %collective-permute-start.7) | collective-permute-done | bytes 1568 | tf_op jit(solution)/shard_map/ppermute | solution.py:472
  25.5 0.0 collective-permute-done.3.odd_ref
  25.5 0.0 collective-permute-done.1.even_ref
  25.5 0.0 collective-permute-done.4.odd_other_ref
  25.5 0.0 collective-permute-done.2.even_other_ref
  25.5 2.2 %shard_map.121 = (f32[10,24,512]{2,1,0:T(8,128)S(1)}, f32[8,24,512]{2,1,0:T(8,128)S(1)}, f32[8,24,512]{2,1,0:T(8,128)S(1)}, f32[8,3,128]{2,1,0:T(4,128)S(1)}) custom-call(f32[2,4,8,512]{3,2,1,0:T(8,128)S(1)} %get-tuple-element.17.own_ref, f32[2,4,8,512]{3,2,1,0:T(8,128)S(1)} %collective-permute-done.other_ref, ...), custom_call_target="tpu_custom_call" | custom-call | tf_op jit(solution)/shard_map/pallas_call | solution.py:404
  27.7 0.0 copy-start
  27.7 10.2 %all_to_all.10.gathered_ref = f32[8,3,128]{2,1,0:T(4,128)S(1)} all-to-all(f32[8,3,128]{2,1,0:T(4,128)S(1)} %get-tuple-element.24), channel_id=1, replica_groups=mesh['grp'=4,'gx'=2,'gy'=4] {'gx','gy'}, dimensions={0} | all-to-all | bytes 24576 | tf_op jit(solution)/shard_map/all_to_all | solution.py:420
  37.9 0.0 copy-start.1
  37.9 1.3 %shard_map.122 = (f32[4,8,128]{2,1,0:T(8,128)S(1)}, f32[4,8,128]{2,1,0:T(8,128)S(1)}, f32[4,8,128]{2,1,0:T(8,128)S(1)}, f32[4,8,128]{2,1,0:T(8,128)S(1)}) custom-call(f32[10,24,512]{2,1,0:T(8,128)S(1)} %get-tuple-element.21.field_ref, f32[8,24,512]{2,1,0:T(8,128)S(1)} %get-tuple-element.22.weight_ref, f32[8,24,512]{2,1,0:T(8,128)S(1)} %get-tuple-element.23.drive_ref, ...), custom_call_target="tpu_custom_call" | custom-call | tf_op jit(solution)/shard_map/pallas_call | solution.py:404
  39.2 0.1 collective-permute-start.8
  39.2 1.6 %collective-permute-start.9 = (f32[4,8,128]{2,1,0:T(8,128)S(1)}, f32[4,8,128]{2,1,0:T(8,128)S(1)}, u32[]{:S(2)}, u32[]{:S(2)}) collective-permute-start(f32[4,8,128]{2,1,0:T(8,128)S(1)} %get-tuple-element.27), channel_id=1, source_target_pairs={{0,16},{8,24},{16,0},{24,8},{1,17},{9,25},{17,1},{25,9},{2,18},{10... | collective-permute-start | bytes 49160 | tf_op jit(solution)/shard_map/ppermute | solution.py:488
  40.8 0.3 collective-permute-start.10
  41.1 0.0 collective-permute-done.8.rest_1_
  41.1 0.0 copy-done
  41.1 0.0 copy-done.1
  41.1 0.5 shard_map.124.early_ref
  41.6 0.0 copy-start.2
  41.6 1.4 %collective-permute-done.9.rest_2_.rest_0_ = f32[4,8,128]{2,1,0:T(8,128)S(1)} collective-permute-done((f32[4,8,128]{2,1,0:T(8,128)S(1)}, f32[4,8,128]{2,1,0:T(8,128)S(1)}, u32[]{:S(2)}, u32[]{:S(2)}) %collective-permute-start.9) | collective-permute-done | bytes 16416 | tf_op jit(solution)/shard_map/ppermute | solution.py:488
  43.0 0.9 %collective-permute-done.10.rest_3_.rest_1_ = f32[4,8,128]{2,1,0:T(8,128)S(1)} collective-permute-done((f32[4,8,128]{2,1,0:T(8,128)S(1)}, f32[4,8,128]{2,1,0:T(8,128)S(1)}, u32[]{:S(2)}, u32[]{:S(2)}) %collective-permute-start.10) | collective-permute-done | bytes 16416 | tf_op jit(solution)/shard_map/ppermute | solution.py:488
  44.0 1.2 %shard_map.125 = f32[32,4,128]{2,1,0:T(4,128)} custom-call(f32[32,4,8,128]{3,2,1,0:T(8,128)S(1)} %copy-done.1, f32[64,4,8,128]{3,2,1,0:T(8,128)S(1)} %copy-done, f32[2,128]{1,0:T(2,128)S(1)} %shard_map.124.early_ref, f32[4,8,128]{2,1,0:T(8,128)S(1)} %collective-permute-done.9.rest_2_.rest_0_, f32[4,8,128]{2,1,0:T(8,128)S(1)} %collective-permute-done.10.rest_3_.rest_1_), custom_call_target="tpu_custom_call" | custom-call | tf_op jit(solution)/shard_map/pallas_call | solution.py:404
  45.1 0.0 copy-start.4
  45.2 2.7 %all-to-all-start.1 = ((f32[32,4,128]{2,1,0:T(4,128)}), f32[32,4,128]{2,1,0:T(4,128)S(1)}, u32[]{:S(2)}, u32[]{:S(2)}) async-start(f32[32,4,128]{2,1,0:T(4,128)} %shard_map.125), calls=%async_computation.1 | async-start | bytes 131072 | tf_op jit(solution)/shard_map/all_to_all | solution.py:420
  47.8 0.0 copy-done.2
  47.9 0.0 copy-done.4
  47.9 0.0 copy-start.3
  47.9 0.0 copy-start.5
  47.9 1.5 %shard_map.123 = f32[32,4,8,128]{3,2,1,0:T(8,128)} custom-call(f32[4,32]{1,0:T(4,128)S(1)} %copy-done.4, f32[32,4,8,128]{3,2,1,0:T(8,128)S(1)} %copy-done.2, f32[4,8,128]{2,1,0:T(8,128)S(1)} %get-tuple-element.25.rest_0_, f32[4,8,128]{2,1,0:T(8,128)S(1)} %collective-permute-done.8.rest_1_, f32[4,8,128]{2,1,0:T(8,128)S(1)} %collective-permute-done.9.rest_2_.rest_0_, ...), custom_call_target="tpu_custom_call" | custom-call | tf_op jit(solution)/shard_map/pallas_call | solution.py:404
  49.4 5.7 %all-to-all-done.1.gathered_ref = f32[32,4,128]{2,1,0:T(4,128)S(1)} async-done(((f32[32,4,128]{2,1,0:T(4,128)}), f32[32,4,128]{2,1,0:T(4,128)S(1)}, u32[]{:S(2)}, u32[]{:S(2)}) %all-to-all-start.1) | async-done | bytes 65568 | tf_op jit(solution)/shard_map/all_to_all | solution.py:420
  55.1 0.0 copy-done.3
  55.1 0.0 copy-done.5
  55.1 0.9 %shard_map.126 = (f32[4,32]{1,0:T(4,128)}, f32[64,64]{1,0:T(8,128)}) custom-call(f32[32,4,128]{2,1,0:T(4,128)S(1)} %all-to-all-done.1.gathered_ref, f32[4,64]{1,0:T(4,128)S(1)} %bitcast.3, f32[64,64]{1,0:T(8,128)S(1)} %copy-done.3), custom_call_target="tpu_custom_call" | custom-call | tf_op jit(solution)/shard_map/pallas_call | solution.py:404
  (3 shorter events, 0.0 us)
Async XLA Ops:
  1.9 8.2 %collective-permute-start = (f32[2,4,8,512]{3,2,1,0:T(8,128)S(1)}, f32[2,4,8,512]{3,2,1,0:T(8,128)S(1)}, u32[]{:S(2)}, u32[]{:S(2)}) collective-permute-start(f32[2,4,8,512]{3,2,1,0:T(8,128)S(1)} %get-tuple-element.17.own_ref), channel_id=1, source_target_pairs={{0,4},{1,5},{2,6},{3,7},{4,0},{5,1},{6,2},{7,3},{8,12},{9,13},{10,... | collective-permute-start | bytes 393224 | tf_op jit(solution)/shard_map/ppermute | solution.py:466
  5.0 20.5 %collective-permute-start.3 = (f32[2,4,8,512]{3,2,1,0:T(8,128)S(1)}, f32[2,4,8,512]{3,2,1,0:T(8,128)S(1)}, u32[]{:S(2)}, u32[]{:S(2)}) collective-permute-start(f32[2,4,8,512]{3,2,1,0:T(8,128)S(1)} %get-tuple-element.17.own_ref), channel_id=1, source_target_pairs={{0,0},{1,2},{2,1},{3,3},{4,4},{5,6},{6,5},{7,7},{8,8},{9,10},{10,9... | collective-permute-start | bytes 393224 | tf_op jit(solution)/shard_map/ppermute | solution.py:466
  5.7 19.8 %collective-permute-start.1 = (f32[2,4,8,512]{3,2,1,0:T(8,128)S(1)}, f32[2,4,8,512]{3,2,1,0:T(8,128)S(1)}, u32[]{:S(2)}, u32[]{:S(2)}) collective-permute-start(f32[2,4,8,512]{3,2,1,0:T(8,128)S(1)} %get-tuple-element.17.own_ref), channel_id=1, source_target_pairs={{0,1},{1,0},{2,3},{3,2},{4,5},{5,4},{6,7},{7,6},{8,9},{9,8},{10,11... | collective-permute-start | bytes 393224 | tf_op jit(solution)/shard_map/ppermute | solution.py:466
  10.1 15.4 %collective-permute-start.4 = (f32[2,4,8,512]{3,2,1,0:T(8,128)S(1)}, f32[2,4,8,512]{3,2,1,0:T(8,128)S(1)}, u32[]{:S(2)}, u32[]{:S(2)}) collective-permute-start(f32[2,4,8,512]{3,2,1,0:T(8,128)S(1)} %collective-permute-done.other_ref), channel_id=1, source_target_pairs={{0,0},{1,2},{2,1},{3,3},{4,4},{5,6},{6,5},{7,7},{8,8},{9,10},{10,9... | collective-permute-start | bytes 393224 | tf_op jit(solution)/shard_map/ppermute | solution.py:466
  10.8 14.7 %collective-permute-start.2 = (f32[2,4,8,512]{3,2,1,0:T(8,128)S(1)}, f32[2,4,8,512]{3,2,1,0:T(8,128)S(1)}, u32[]{:S(2)}, u32[]{:S(2)}) collective-permute-start(f32[2,4,8,512]{3,2,1,0:T(8,128)S(1)} %collective-permute-done.other_ref), channel_id=1, source_target_pairs={{0,1},{1,0},{2,3},{3,2},{4,5},{5,4},{6,7},{7,6},{8,9},{9,8},{10,11... | collective-permute-start | bytes 393224 | tf_op jit(solution)/shard_map/ppermute | solution.py:466
  13.8 4.5 %collective-permute-start.5 = (f32[3,128]{1,0:T(4,128)S(1)}, f32[3,128]{1,0:T(4,128)S(1)}, u32[]{:S(2)}, u32[]{:S(2)}) collective-permute-start(f32[3,128]{1,0:T(4,128)S(1)} %get-tuple-element.20), channel_id=1, source_target_pairs={{0,2},{1,3},{2,0},{3,1},{4,6},{5,7},{6,4},{7,5},{8,10},{9,11},{10,... | collective-permute-start | bytes 4616 | tf_op jit(solution)/shard_map/ppermute | solution.py:472
  18.3 3.6 %collective-permute-start.6 = (f32[3,128]{1,0:T(4,128)S(1)}, f32[3,128]{1,0:T(4,128)S(1)}, u32[]{:S(2)}, u32[]{:S(2)}) collective-permute-start(f32[3,128]{1,0:T(4,128)S(1)} %add.9), channel_id=1, source_target_pairs={{0,4},{4,0},{1,5},{5,1},{2,6},{6,2},{3,7},{7,3},{8,12},{12,8},{9,1... | collective-permute-start | bytes 4616 | tf_op jit(solution)/shard_map/ppermute | solution.py:472
  21.9 3.6 %collective-permute-start.7 = (f32[3,128]{1,0:T(4,128)S(1)}, f32[3,128]{1,0:T(4,128)S(1)}, u32[]{:S(2)}, u32[]{:S(2)}) collective-permute-start(f32[3,128]{1,0:T(4,128)S(1)} %add.10), channel_id=1, source_target_pairs={{0,1},{1,0},{2,3},{3,2},{4,5},{5,4},{6,7},{7,6},{8,9},{9,8},{10,11... | collective-permute-start | bytes 4616 | tf_op jit(solution)/shard_map/ppermute | solution.py:472
  27.7 13.4 %copy-start = (f32[64,4,8,128]{3,2,1,0:T(8,128)S(1)}, f32[64,4,8,128]{3,2,1,0:T(8,128)}, u32[]{:S(2)}) copy-start(f32[64,4,8,128]{3,2,1,0:T(8,128)} %phi_ref.3) | copy-start | bytes 3145732
  37.9 3.2 %copy-start.1 = (f32[32,4,8,128]{3,2,1,0:T(8,128)S(1)}, f32[32,4,8,128]{3,2,1,0:T(8,128)}, u32[]{:S(2)}) copy-start(f32[32,4,8,128]{3,2,1,0:T(8,128)} %psi_ref.3) | copy-start | bytes 1572868
  39.2 1.9 %collective-permute-start.8 = (f32[4,8,128]{2,1,0:T(8,128)S(1)}, f32[4,8,128]{2,1,0:T(8,128)S(1)}, u32[]{:S(2)}, u32[]{:S(2)}) collective-permute-start(f32[4,8,128]{2,1,0:T(8,128)S(1)} %get-tuple-element.26), channel_id=1, source_target_pairs={{0,8},{8,0},{16,24},{24,16},{1,9},{9,1},{17,25},{25,17},{2,10},{10... | collective-permute-start | bytes 49160 | tf_op jit(solution)/shard_map/ppermute | solution.py:488
  39.2 3.8 %collective-permute-start.9 = (f32[4,8,128]{2,1,0:T(8,128)S(1)}, f32[4,8,128]{2,1,0:T(8,128)S(1)}, u32[]{:S(2)}, u32[]{:S(2)}) collective-permute-start(f32[4,8,128]{2,1,0:T(8,128)S(1)} %get-tuple-element.27), channel_id=1, source_target_pairs={{0,16},{8,24},{16,0},{24,8},{1,17},{9,25},{17,1},{25,9},{2,18},{10... | collective-permute-start | bytes 49160 | tf_op jit(solution)/shard_map/ppermute | solution.py:488
  40.8 3.2 %collective-permute-start.10 = (f32[4,8,128]{2,1,0:T(8,128)S(1)}, f32[4,8,128]{2,1,0:T(8,128)S(1)}, u32[]{:S(2)}, u32[]{:S(2)}) collective-permute-start(f32[4,8,128]{2,1,0:T(8,128)S(1)} %get-tuple-element.28), channel_id=1, source_target_pairs={{0,24},{8,16},{16,8},{24,0},{1,25},{9,17},{17,9},{25,1},{2,26},{10... | collective-permute-start | bytes 49160 | tf_op jit(solution)/shard_map/ppermute | solution.py:488
  41.6 6.2 %copy-start.2 = (f32[32,4,8,128]{3,2,1,0:T(8,128)S(1)}, f32[32,4,8,128]{3,2,1,0:T(8,128)}, u32[]{:S(2)}) copy-start(f32[32,4,8,128]{3,2,1,0:T(8,128)} %range_ref.1) | copy-start | bytes 1572868
  45.1 2.7 %copy-start.4 = (f32[4,32]{1,0:T(4,128)S(1)}, f32[4,32]{1,0:T(4,128)}, u32[]{:S(2)}) copy-start(f32[4,32]{1,0:T(4,128)} %omega_ref.1) | copy-start | bytes 1540
  45.2 10.0 %all-to-all-start.1 = ((f32[32,4,128]{2,1,0:T(4,128)}), f32[32,4,128]{2,1,0:T(4,128)S(1)}, u32[]{:S(2)}, u32[]{:S(2)}) async-start(f32[32,4,128]{2,1,0:T(4,128)} %shard_map.125), calls=%async_computation.1 | async-start | bytes 131072 | tf_op jit(solution)/shard_map/all_to_all | solution.py:420
  47.9 7.3 %copy-start.3 = (f32[64,64]{1,0:T(8,128)S(1)}, f32[64,64]{1,0:T(8,128)}, u32[]{:S(2)}) copy-start(f32[64,64]{1,0:T(8,128)} %core_ref.1) | copy-start | bytes 49156
  47.9 7.2 %copy-start.5 = (f32[64,4]{0,1:T(4,128)S(1)}, f32[64,4]{0,1:T(4,128)}, u32[]{:S(2)}) copy-start(f32[64,4]{0,1:T(4,128)} %param.17) | copy-start | bytes 3076
where the time goes:
time: 56.3 us; the launch traced here: 56.1 us
  starting transfers between devices  18.4 us (33%)
  waiting for transfers between devices  17.8 us (32%)
  blocking collectives  10.2 us (18%)
  Pallas kernels  8.93 us (16%)
  between operations  0.76 us (1%)
    ppermute x5, starting transfers between devices, fast_body(): others.append(lax.ppermute(sent, ('gx', 'gy'), pairs(cross, phase)))  11.9 us
    all_to_all x1, blocking collectives, gather(): return lax.all_to_all(copies, axes, 0, 0)  10.2 us
    ppermute x3, waiting for transfers between devices, fast_body(): lax.ppermute(gathered, axis, [(i, i ^ bit) for i in range(count)])  9.74 us
    pallas_call x6, Pallas kernels, call(): pl.pallas_call(kernel, out_shape=shapes, in_specs=specs or [vmem] * len(i...  7.64 us
    all_to_all x1, waiting for transfers between devices, gather(): return lax.all_to_all(copies, axes, 0, 0)  5.7 us
    all_to_all x1, starting transfers between devices, gather(): return lax.all_to_all(copies, axes, 0, 0)  2.68 us
    ppermute x3, waiting for transfers between devices, fast_body(): lax.ppermute(pieces[turn], 'grp', [(at, at ^ turn) for at in range(groups)])  2.33 us
    ppermute x3, starting transfers between devices, fast_body(): lax.ppermute(pieces[turn], 'grp', [(at, at ^ turn) for at in range(groups)])  1.92 us
  transfers between devices with their start and end apart: 12, of which 6 were waited for; matrix products, arithmetic and copies ran while one was open for 0% of the time, Pallas kernels for 4%

commit v1 on v0

--- a/solution.py
+++ b/solution.py
@@ -435,13 +435,19 @@
     padded = (window[0] + 2,) + window[1:]
     copies = (count_x * count_y, coarse // LANES + 1, LANES)
 
-    def partner_y(at, phase):
-        found = at ^ 1 if phase == 0 else ((at + 1) ^ 1) - 1
-        return found if 0 <= found < count_y else at
-
-    def pairs(cross, phase):
+    def place(group, x, y):
+        return (group * count_x + x) * count_y + y
+
+    def partner(group, x, y, phase):
+        if phase is None:
+            return place(group, x ^ 1, y)
+        beyond = y ^ 1 if phase == 0 else ((y + 1) ^ 1) - 1
+        return place(group, x, beyond) if 0 <= beyond < count_y else place(group ^ 1, x, y)
+
+    def pairs(phase):
         return [
-            (x * count_y + y, (x ^ cross) * count_y + (y if phase is None else partner_y(y, phase)))
+            (place(group, x, y), partner(group, x, y, phase))
+            for group in range(groups)
             for x in range(count_x)
             for y in range(count_y)
         ]
@@ -461,9 +467,9 @@
         name="begin",
     )(*map(in_hbm, (source, diagonal, coarse_ids, coarse_inverse)))
     others = []
-    for at, (cross, phase) in enumerate(((1, None), (0, 0), (0, 0), (0, 1), (0, 1))):
+    for at, phase in enumerate((None, 0, 0, 1, 1)):
         sent = others[0] if at in (2, 4) else mine
-        others.append(lax.ppermute(sent, ("gx", "gy"), pairs(cross, phase)))
+        others.append(lax.ppermute(sent, ("grp", "gx", "gy"), pairs(phase)))
     gathered = begin
     bits = [1 << bit for bit in reversed(range(count_y.bit_length() - 1))]
     turns = [("gy", count_y, bit) for bit in bits]

time: 56.3 us -> 54.4 us (0.966)
  waiting for transfers between devices: 17.8 us -> 16.8 us
  starting transfers between devices: 18.4 us -> 17.5 us
    ppermute x5, starting transfers between devices: 11.9 us -> 9.58 us  [fast_body(): others.append(lax.ppermute(sent, ('grp', 'gx', 'gy'), pairs(phase)))]
    ppermute x3, starting transfers between devices: 1.91 us -> 3.28 us  [fast_body(): lax.ppermute(gathered, axis, [(i, i ^ bit) for i in range(count)])]
    ppermute x3, waiting for transfers between devices: 9.74 us -> 8.37 us  [fast_body(): lax.ppermute(gathered, axis, [(i, i ^ bit) for i in range(count)])]
  transfers between devices with their start and end apart: 12 -> 12, of which waited for: 6 -> 7; matrix products, arithmetic and copies ran while one was open for 0% -> 0% of each run, Pallas kernels for 4% -> 4%
where the time goes in v1:
time: 54.4 us; the launch traced here: 54.1 us
  starting transfers between devices  17.5 us (32%)
  waiting for transfers between devices  16.8 us (31%)
  blocking collectives  10.2 us (19%)
  Pallas kernels  8.93 us (16%)
  between operations  0.74 us (1%)
    all_to_all x1, blocking collectives, gather(): return lax.all_to_all(copies, axes, 0, 0)  10.2 us
    ppermute x5, starting transfers between devices, fast_body(): others.append(lax.ppermute(sent, ('grp', 'gx', 'gy'), pairs(phase)))  9.58 us
    ppermute x3, waiting for transfers between devices, fast_body(): lax.ppermute(gathered, axis, [(i, i ^ bit) for i in range(count)])  8.37 us
    pallas_call x6, Pallas kernels, call(): pl.pallas_call(kernel, out_shape=shapes, in_specs=specs or [vmem] * len(i...  7.64 us
    all_to_all x1, waiting for transfers between devices, gather(): return lax.all_to_all(copies, axes, 0, 0)  5.7 us
    ppermute x3, starting transfers between devices, fast_body(): lax.ppermute(gathered, axis, [(i, i ^ bit) for i in range(count)])  3.28 us
    all_to_all x1, starting transfers between devices, gather(): return lax.all_to_all(copies, axes, 0, 0)  2.68 us
    ppermute x3, waiting for transfers between devices, fast_body(): lax.ppermute(pieces[turn], 'grp', [(at, at ^ turn) for at in range(groups)])  2.33 us
  transfers between devices with their start and end apart: 12, of which 7 were waited for; matrix products, arithmetic and copies ran while one was open for 0% of the time, Pallas kernels for 4%

profile of v1, /device:TPU:0, one launch (start us, length us, event | category | flops | bytes accessed | tf_op | source)
XLA Modules:
  0.0 54.1 jit_solution(1328826598560643150)
XLA Ops:
  0.6 1.3 %begin.1 = (f32[2,4,8,512]{3,2,1,0:T(8,128)S(1)}, s32[4,8,512]{2,1,0:T(8,128)S(1)}, f32[256,256]{1,0:T(8,128)S(1)}, f32[3,128]{1,0:T(4,128)S(1)}) custom-call(f32[4,8,512]{2,1,0:T(8,128)} %bitcast.4, f32[4,8,512]{2,1,0:T(8,128)} %diagonal_from.1, s32[4,8,512]{2,1,0:T(8,128)} %ids_from.1, f32[256,256]{1,0:T(8,128)} %inverse_from.1), custom_call_target="tpu_custom_call" | custom-call | tf_op jit(solution)/shard_map/begin/pallas_call | solution.py:455
  1.9 3.1 %collective-permute-start = (f32[2,4,8,512]{3,2,1,0:T(8,128)S(1)}, f32[2,4,8,512]{3,2,1,0:T(8,128)S(1)}, u32[]{:S(2)}, u32[]{:S(2)}) collective-permute-start(f32[2,4,8,512]{3,2,1,0:T(8,128)S(1)} %get-tuple-element.17.own_ref), channel_id=1, source_target_pairs={{0,4},{1,5},{2,6},{3,7},{4,0},{5,1},{6,2},{7,3},{8,12},{9,13},{10,... | collective-permute-start | bytes 393224 | tf_op jit(solution)/shard_map/ppermute | solution.py:472
  5.0 0.0 collective-permute-start.3
  5.0 3.1 %collective-permute-start.1 = (f32[2,4,8,512]{3,2,1,0:T(8,128)S(1)}, f32[2,4,8,512]{3,2,1,0:T(8,128)S(1)}, u32[]{:S(2)}, u32[]{:S(2)}) collective-permute-start(f32[2,4,8,512]{3,2,1,0:T(8,128)S(1)} %get-tuple-element.17.own_ref), channel_id=1, source_target_pairs={{0,1},{1,0},{2,3},{3,2},{4,5},{5,4},{6,7},{7,6},{8,9},{9,8},{10,11... | collective-permute-start | bytes 393224 | tf_op jit(solution)/shard_map/ppermute | solution.py:472
  8.1 0.3 collective-permute-done.other_ref
  8.5 0.0 collective-permute-start.4
  8.5 3.4 %collective-permute-start.2 = (f32[2,4,8,512]{3,2,1,0:T(8,128)S(1)}, f32[2,4,8,512]{3,2,1,0:T(8,128)S(1)}, u32[]{:S(2)}, u32[]{:S(2)}) collective-permute-start(f32[2,4,8,512]{3,2,1,0:T(8,128)S(1)} %collective-permute-done.other_ref), channel_id=1, source_target_pairs={{0,1},{1,0},{2,3},{3,2},{4,5},{5,4},{6,7},{7,6},{8,9},{9,8},{10,11... | collective-permute-start | bytes 393224 | tf_op jit(solution)/shard_map/ppermute | solution.py:472
  11.9 1.0 %collective-permute-start.5 = (f32[3,128]{1,0:T(4,128)S(1)}, f32[3,128]{1,0:T(4,128)S(1)}, u32[]{:S(2)}, u32[]{:S(2)}) collective-permute-start(f32[3,128]{1,0:T(4,128)S(1)} %get-tuple-element.20), channel_id=1, source_target_pairs={{0,2},{1,3},{2,0},{3,1},{4,6},{5,7},{6,4},{7,5},{8,10},{9,11},{10,... | collective-permute-start | bytes 4616 | tf_op jit(solution)/shard_map/ppermute | solution.py:478
  12.9 3.5 %collective-permute-done.5 = f32[3,128]{1,0:T(4,128)S(1)} collective-permute-done((f32[3,128]{1,0:T(4,128)S(1)}, f32[3,128]{1,0:T(4,128)S(1)}, u32[]{:S(2)}, u32[]{:S(2)}) %collective-permute-start.5) | collective-permute-done | bytes 1568 | tf_op jit(solution)/shard_map/ppermute | solution.py:478
  16.3 1.5 %collective-permute-start.6 = (f32[3,128]{1,0:T(4,128)S(1)}, f32[3,128]{1,0:T(4,128)S(1)}, u32[]{:S(2)}, u32[]{:S(2)}) collective-permute-start(f32[3,128]{1,0:T(4,128)S(1)} %add.9), channel_id=1, source_target_pairs={{0,4},{4,0},{1,5},{5,1},{2,6},{6,2},{3,7},{7,3},{8,12},{12,8},{9,1... | collective-permute-start | bytes 4616 | tf_op jit(solution)/shard_map/ppermute | solution.py:478
  17.9 2.1 %collective-permute-done.6 = f32[3,128]{1,0:T(4,128)S(1)} collective-permute-done((f32[3,128]{1,0:T(4,128)S(1)}, f32[3,128]{1,0:T(4,128)S(1)}, u32[]{:S(2)}, u32[]{:S(2)}) %collective-permute-start.6) | collective-permute-done | bytes 1568 | tf_op jit(solution)/shard_map/ppermute | solution.py:478
  19.9 0.7 %collective-permute-start.7 = (f32[3,128]{1,0:T(4,128)S(1)}, f32[3,128]{1,0:T(4,128)S(1)}, u32[]{:S(2)}, u32[]{:S(2)}) collective-permute-start(f32[3,128]{1,0:T(4,128)S(1)} %add.10), channel_id=1, source_target_pairs={{0,1},{1,0},{2,3},{3,2},{4,5},{5,4},{6,7},{7,6},{8,9},{9,8},{10,11... | collective-permute-start | bytes 4616 | tf_op jit(solution)/shard_map/ppermute | solution.py:478
  20.7 2.8 %collective-permute-done.7 = f32[3,128]{1,0:T(4,128)S(1)} collective-permute-done((f32[3,128]{1,0:T(4,128)S(1)}, f32[3,128]{1,0:T(4,128)S(1)}, u32[]{:S(2)}, u32[]{:S(2)}) %collective-permute-start.7) | collective-permute-done | bytes 1568 | tf_op jit(solution)/shard_map/ppermute | solution.py:478
  23.5 0.0 collective-permute-done.3.odd_ref
  23.5 0.0 collective-permute-done.1.even_ref
  23.5 0.0 collective-permute-done.4.odd_other_ref
  23.5 0.0 collective-permute-done.2.even_other_ref
  23.6 2.2 %shard_map.121 = (f32[10,24,512]{2,1,0:T(8,128)S(1)}, f32[8,24,512]{2,1,0:T(8,128)S(1)}, f32[8,24,512]{2,1,0:T(8,128)S(1)}, f32[8,3,128]{2,1,0:T(4,128)S(1)}) custom-call(f32[2,4,8,512]{3,2,1,0:T(8,128)S(1)} %get-tuple-element.17.own_ref, f32[2,4,8,512]{3,2,1,0:T(8,128)S(1)} %collective-permute-done.other_ref, ...), custom_call_target="tpu_custom_call" | custom-call | tf_op jit(solution)/shard_map/pallas_call | solution.py:404
  25.7 0.0 copy-start
  25.8 10.2 %all_to_all.10.gathered_ref = f32[8,3,128]{2,1,0:T(4,128)S(1)} all-to-all(f32[8,3,128]{2,1,0:T(4,128)S(1)} %get-tuple-element.24), channel_id=1, replica_groups=mesh['grp'=4,'gx'=2,'gy'=4] {'gx','gy'}, dimensions={0} | all-to-all | bytes 24576 | tf_op jit(solution)/shard_map/all_to_all | solution.py:420
  36.0 0.0 copy-start.1
  36.0 1.3 %shard_map.122 = (f32[4,8,128]{2,1,0:T(8,128)S(1)}, f32[4,8,128]{2,1,0:T(8,128)S(1)}, f32[4,8,128]{2,1,0:T(8,128)S(1)}, f32[4,8,128]{2,1,0:T(8,128)S(1)}) custom-call(f32[10,24,512]{2,1,0:T(8,128)S(1)} %get-tuple-element.21.field_ref, f32[8,24,512]{2,1,0:T(8,128)S(1)} %get-tuple-element.22.weight_ref, f32[8,24,512]{2,1,0:T(8,128)S(1)} %get-tuple-element.23.drive_ref, ...), custom_call_target="tpu_custom_call" | custom-call | tf_op jit(solution)/shard_map/pallas_call | solution.py:404
  37.2 0.1 collective-permute-start.8
  37.3 1.6 %collective-permute-start.9 = (f32[4,8,128]{2,1,0:T(8,128)S(1)}, f32[4,8,128]{2,1,0:T(8,128)S(1)}, u32[]{:S(2)}, u32[]{:S(2)}) collective-permute-start(f32[4,8,128]{2,1,0:T(8,128)S(1)} %get-tuple-element.27), channel_id=1, source_target_pairs={{0,16},{8,24},{16,0},{24,8},{1,17},{9,25},{17,1},{25,9},{2,18},{10... | collective-permute-start | bytes 49160 | tf_op jit(solution)/shard_map/ppermute | solution.py:494
  38.9 0.3 collective-permute-start.10
  39.2 0.0 collective-permute-done.8.rest_1_
  39.2 0.0 copy-done
  39.2 0.0 copy-done.1
  39.2 0.5 shard_map.124.early_ref
  39.7 0.0 copy-start.2
  39.7 1.4 %collective-permute-done.9.rest_2_.rest_0_ = f32[4,8,128]{2,1,0:T(8,128)S(1)} collective-permute-done((f32[4,8,128]{2,1,0:T(8,128)S(1)}, f32[4,8,128]{2,1,0:T(8,128)S(1)}, u32[]{:S(2)}, u32[]{:S(2)}) %collective-permute-start.9) | collective-permute-done | bytes 16416 | tf_op jit(solution)/shard_map/ppermute | solution.py:494
  41.1 0.9 %collective-permute-done.10.rest_3_.rest_1_ = f32[4,8,128]{2,1,0:T(8,128)S(1)} collective-permute-done((f32[4,8,128]{2,1,0:T(8,128)S(1)}, f32[4,8,128]{2,1,0:T(8,128)S(1)}, u32[]{:S(2)}, u32[]{:S(2)}) %collective-permute-start.10) | collective-permute-done | bytes 16416 | tf_op jit(solution)/shard_map/ppermute | solution.py:494
  42.0 1.2 %shard_map.125 = f32[32,4,128]{2,1,0:T(4,128)} custom-call(f32[32,4,8,128]{3,2,1,0:T(8,128)S(1)} %copy-done.1, f32[64,4,8,128]{3,2,1,0:T(8,128)S(1)} %copy-done, f32[2,128]{1,0:T(2,128)S(1)} %shard_map.124.early_ref, f32[4,8,128]{2,1,0:T(8,128)S(1)} %collective-permute-done.9.rest_2_.rest_0_, f32[4,8,128]{2,1,0:T(8,128)S(1)} %collective-permute-done.10.rest_3_.rest_1_), custom_call_target="tpu_custom_call" | custom-call | tf_op jit(solution)/shard_map/pallas_call | solution.py:404
  43.2 0.0 copy-start.4
  43.2 2.7 %all-to-all-start.1 = ((f32[32,4,128]{2,1,0:T(4,128)}), f32[32,4,128]{2,1,0:T(4,128)S(1)}, u32[]{:S(2)}, u32[]{:S(2)}) async-start(f32[32,4,128]{2,1,0:T(4,128)} %shard_map.125), calls=%async_computation.1 | async-start | bytes 131072 | tf_op jit(solution)/shard_map/all_to_all | solution.py:420
  45.9 0.0 copy-done.2
  45.9 0.0 copy-done.4
  45.9 0.0 copy-start.3
  45.9 0.0 copy-start.5
  46.0 1.5 %shard_map.123 = f32[32,4,8,128]{3,2,1,0:T(8,128)} custom-call(f32[4,32]{1,0:T(4,128)S(1)} %copy-done.4, f32[32,4,8,128]{3,2,1,0:T(8,128)S(1)} %copy-done.2, f32[4,8,128]{2,1,0:T(8,128)S(1)} %get-tuple-element.25.rest_0_, f32[4,8,128]{2,1,0:T(8,128)S(1)} %collective-permute-done.8.rest_1_, f32[4,8,128]{2,1,0:T(8,128)S(1)} %collective-permute-done.9.rest_2_.rest_0_, ...), custom_call_target="tpu_custom_call" | custom-call | tf_op jit(solution)/shard_map/pallas_call | solution.py:404
  47.5 5.7 %all-to-all-done.1.gathered_ref = f32[32,4,128]{2,1,0:T(4,128)S(1)} async-done(((f32[32,4,128]{2,1,0:T(4,128)}), f32[32,4,128]{2,1,0:T(4,128)S(1)}, u32[]{:S(2)}, u32[]{:S(2)}) %all-to-all-start.1) | async-done | bytes 65568 | tf_op jit(solution)/shard_map/all_to_all | solution.py:420
  53.2 0.0 copy-done.3
  53.2 0.0 copy-done.5
  53.2 0.9 %shard_map.126 = (f32[4,32]{1,0:T(4,128)}, f32[64,64]{1,0:T(8,128)}) custom-call(f32[32,4,128]{2,1,0:T(4,128)S(1)} %all-to-all-done.1.gathered_ref, f32[4,64]{1,0:T(4,128)S(1)} %bitcast.3, f32[64,64]{1,0:T(8,128)S(1)} %copy-done.3), custom_call_target="tpu_custom_call" | custom-call | tf_op jit(solution)/shard_map/pallas_call | solution.py:404
  (3 shorter events, 0.0 us)
Async XLA Ops:
  1.9 6.6 %collective-permute-start = (f32[2,4,8,512]{3,2,1,0:T(8,128)S(1)}, f32[2,4,8,512]{3,2,1,0:T(8,128)S(1)}, u32[]{:S(2)}, u32[]{:S(2)}) collective-permute-start(f32[2,4,8,512]{3,2,1,0:T(8,128)S(1)} %get-tuple-element.17.own_ref), channel_id=1, source_target_pairs={{0,4},{1,5},{2,6},{3,7},{4,0},{5,1},{6,2},{7,3},{8,12},{9,13},{10,... | collective-permute-start | bytes 393224 | tf_op jit(solution)/shard_map/ppermute | solution.py:472
  5.0 18.5 %collective-permute-start.3 = (f32[2,4,8,512]{3,2,1,0:T(8,128)S(1)}, f32[2,4,8,512]{3,2,1,0:T(8,128)S(1)}, u32[]{:S(2)}, u32[]{:S(2)}) collective-permute-start(f32[2,4,8,512]{3,2,1,0:T(8,128)S(1)} %get-tuple-element.17.own_ref), channel_id=1, source_target_pairs={{0,8},{1,2},{2,1},{3,11},{4,12},{5,6},{6,5},{7,15},{8,0},{9,10},{1... | collective-permute-start | bytes 393224 | tf_op jit(solution)/shard_map/ppermute | solution.py:472
  5.0 18.5 %collective-permute-start.1 = (f32[2,4,8,512]{3,2,1,0:T(8,128)S(1)}, f32[2,4,8,512]{3,2,1,0:T(8,128)S(1)}, u32[]{:S(2)}, u32[]{:S(2)}) collective-permute-start(f32[2,4,8,512]{3,2,1,0:T(8,128)S(1)} %get-tuple-element.17.own_ref), channel_id=1, source_target_pairs={{0,1},{1,0},{2,3},{3,2},{4,5},{5,4},{6,7},{7,6},{8,9},{9,8},{10,11... | collective-permute-start | bytes 393224 | tf_op jit(solution)/shard_map/ppermute | solution.py:472
  8.5 15.1 %collective-permute-start.4 = (f32[2,4,8,512]{3,2,1,0:T(8,128)S(1)}, f32[2,4,8,512]{3,2,1,0:T(8,128)S(1)}, u32[]{:S(2)}, u32[]{:S(2)}) collective-permute-start(f32[2,4,8,512]{3,2,1,0:T(8,128)S(1)} %collective-permute-done.other_ref), channel_id=1, source_target_pairs={{0,8},{1,2},{2,1},{3,11},{4,12},{5,6},{6,5},{7,15},{8,0},{9,10},{1... | collective-permute-start | bytes 393224 | tf_op jit(solution)/shard_map/ppermute | solution.py:472
  8.5 15.1 %collective-permute-start.2 = (f32[2,4,8,512]{3,2,1,0:T(8,128)S(1)}, f32[2,4,8,512]{3,2,1,0:T(8,128)S(1)}, u32[]{:S(2)}, u32[]{:S(2)}) collective-permute-start(f32[2,4,8,512]{3,2,1,0:T(8,128)S(1)} %collective-permute-done.other_ref), channel_id=1, source_target_pairs={{0,1},{1,0},{2,3},{3,2},{4,5},{5,4},{6,7},{7,6},{8,9},{9,8},{10,11... | collective-permute-start | bytes 393224 | tf_op jit(solution)/shard_map/ppermute | solution.py:472
  11.9 4.5 %collective-permute-start.5 = (f32[3,128]{1,0:T(4,128)S(1)}, f32[3,128]{1,0:T(4,128)S(1)}, u32[]{:S(2)}, u32[]{:S(2)}) collective-permute-start(f32[3,128]{1,0:T(4,128)S(1)} %get-tuple-element.20), channel_id=1, source_target_pairs={{0,2},{1,3},{2,0},{3,1},{4,6},{5,7},{6,4},{7,5},{8,10},{9,11},{10,... | collective-permute-start | bytes 4616 | tf_op jit(solution)/shard_map/ppermute | solution.py:478
  16.3 3.6 %collective-permute-start.6 = (f32[3,128]{1,0:T(4,128)S(1)}, f32[3,128]{1,0:T(4,128)S(1)}, u32[]{:S(2)}, u32[]{:S(2)}) collective-permute-start(f32[3,128]{1,0:T(4,128)S(1)} %add.9), channel_id=1, source_target_pairs={{0,4},{4,0},{1,5},{5,1},{2,6},{6,2},{3,7},{7,3},{8,12},{12,8},{9,1... | collective-permute-start | bytes 4616 | tf_op jit(solution)/shard_map/ppermute | solution.py:478
  19.9 3.6 %collective-permute-start.7 = (f32[3,128]{1,0:T(4,128)S(1)}, f32[3,128]{1,0:T(4,128)S(1)}, u32[]{:S(2)}, u32[]{:S(2)}) collective-permute-start(f32[3,128]{1,0:T(4,128)S(1)} %add.10), channel_id=1, source_target_pairs={{0,1},{1,0},{2,3},{3,2},{4,5},{5,4},{6,7},{7,6},{8,9},{9,8},{10,11... | collective-permute-start | bytes 4616 | tf_op jit(solution)/shard_map/ppermute | solution.py:478
  25.7 13.4 %copy-start = (f32[64,4,8,128]{3,2,1,0:T(8,128)S(1)}, f32[64,4,8,128]{3,2,1,0:T(8,128)}, u32[]{:S(2)}) copy-start(f32[64,4,8,128]{3,2,1,0:T(8,128)} %phi_ref.3) | copy-start | bytes 3145732
  36.0 3.2 %copy-start.1 = (f32[32,4,8,128]{3,2,1,0:T(8,128)S(1)}, f32[32,4,8,128]{3,2,1,0:T(8,128)}, u32[]{:S(2)}) copy-start(f32[32,4,8,128]{3,2,1,0:T(8,128)} %psi_ref.3) | copy-start | bytes 1572868
  37.2 1.9 %collective-permute-start.8 = (f32[4,8,128]{2,1,0:T(8,128)S(1)}, f32[4,8,128]{2,1,0:T(8,128)S(1)}, u32[]{:S(2)}, u32[]{:S(2)}) collective-permute-start(f32[4,8,128]{2,1,0:T(8,128)S(1)} %get-tuple-element.26), channel_id=1, source_target_pairs={{0,8},{8,0},{16,24},{24,16},{1,9},{9,1},{17,25},{25,17},{2,10},{10... | collective-permute-start | bytes 49160 | tf_op jit(solution)/shard_map/ppermute | solution.py:494
  37.3 3.8 %collective-permute-start.9 = (f32[4,8,128]{2,1,0:T(8,128)S(1)}, f32[4,8,128]{2,1,0:T(8,128)S(1)}, u32[]{:S(2)}, u32[]{:S(2)}) collective-permute-start(f32[4,8,128]{2,1,0:T(8,128)S(1)} %get-tuple-element.27), channel_id=1, source_target_pairs={{0,16},{8,24},{16,0},{24,8},{1,17},{9,25},{17,1},{25,9},{2,18},{10... | collective-permute-start | bytes 49160 | tf_op jit(solution)/shard_map/ppermute | solution.py:494
  38.9 3.2 %collective-permute-start.10 = (f32[4,8,128]{2,1,0:T(8,128)S(1)}, f32[4,8,128]{2,1,0:T(8,128)S(1)}, u32[]{:S(2)}, u32[]{:S(2)}) collective-permute-start(f32[4,8,128]{2,1,0:T(8,128)S(1)} %get-tuple-element.28), channel_id=1, source_target_pairs={{0,24},{8,16},{16,8},{24,0},{1,25},{9,17},{17,9},{25,1},{2,26},{10... | collective-permute-start | bytes 49160 | tf_op jit(solution)/shard_map/ppermute | solution.py:494
  39.7 6.2 %copy-start.2 = (f32[32,4,8,128]{3,2,1,0:T(8,128)S(1)}, f32[32,4,8,128]{3,2,1,0:T(8,128)}, u32[]{:S(2)}) copy-start(f32[32,4,8,128]{3,2,1,0:T(8,128)} %range_ref.1) | copy-start | bytes 1572868
  43.2 2.7 %copy-start.4 = (f32[4,32]{1,0:T(4,128)S(1)}, f32[4,32]{1,0:T(4,128)}, u32[]{:S(2)}) copy-start(f32[4,32]{1,0:T(4,128)} %omega_ref.1) | copy-start | bytes 1540
  43.2 10.0 %all-to-all-start.1 = ((f32[32,4,128]{2,1,0:T(4,128)}), f32[32,4,128]{2,1,0:T(4,128)S(1)}, u32[]{:S(2)}, u32[]{:S(2)}) async-start(f32[32,4,128]{2,1,0:T(4,128)} %shard_map.125), calls=%async_computation.1 | async-start | bytes 131072 | tf_op jit(solution)/shard_map/all_to_all | solution.py:420
  45.9 7.3 %copy-start.3 = (f32[64,64]{1,0:T(8,128)S(1)}, f32[64,64]{1,0:T(8,128)}, u32[]{:S(2)}) copy-start(f32[64,64]{1,0:T(8,128)} %core_ref.1) | copy-start | bytes 49156
  45.9 7.2 %copy-start.5 = (f32[64,4]{0,1:T(4,128)S(1)}, f32[64,4]{0,1:T(4,128)}, u32[]{:S(2)}) copy-start(f32[64,4]{0,1:T(4,128)} %param.17) | copy-start | bytes 3076

commit v2 on v1

--- a/solution.py
+++ b/solution.py
@@ -473,7 +473,7 @@
     gathered = begin
     bits = [1 << bit for bit in reversed(range(count_y.bit_length() - 1))]
     turns = [("gy", count_y, bit) for bit in bits]
-    turns.insert(1, ("gx", count_x, 1))
+    turns.append(("gx", count_x, 1))
     for axis, count, bit in turns:
         gathered = gathered + lax.ppermute(gathered, axis, [(i, i ^ bit) for i in range(count)])
     field, weight, drive, partial = call(
@@ -545,6 +545,10 @@
     return center + jacobi_weight * (source - applied) / (6.0 + diagonal)
 
 
+def widen_faces(values):
+    return with_halo(values, (("gx", 0), ("gy", 1)), 1)
+
+
 def axis_maps(coarse_ids):
     ranks_x = coarse_ids[:, 0, 0] // (XY_CUTS * Z_CUTS)
     ranks_y = coarse_ids[0, :, 0] // Z_CUTS % XY_CUTS
@@ -577,7 +581,15 @@
 
 
 def general_body(
-    sources, diagonal, coarse_ids, coarse_inverse, omega_rows, psi, phi, xi_cols, range_sketch,
+    sources,
+    diagonal,
+    coarse_ids,
+    coarse_inverse,
+    omega_rows,
+    psi,
+    phi,
+    xi_cols,
+    range_sketch,
     core_sketch,
 ):
     source = sources[0]
@@ -586,18 +598,29 @@
     total_cells = rows_x * lax.axis_size("gx") * rows_y * lax.axis_size("gy") * cells_z
     scale_factor = coarse / total_cells
     maps = axis_maps(coarse_ids)
-    sides = (("gx", 0), ("gy", 1))
+    stacked = jnp.stack([source, diagonal])
+    margin = with_halo(stacked, (("gx", 1), ("gy", 2)), 2)
+    place_x = lax.axis_index("gx") * rows_x + jnp.arange(rows_x + 4) - 2
+    place_y = lax.axis_index("gy") * rows_y + jnp.arange(rows_y + 4) - 2
+    inside_x = ((place_x >= 0) & (place_x < rows_x * lax.axis_size("gx"))).astype(jnp.float32)
+    inside_y = ((place_y >= 0) & (place_y < rows_y * lax.axis_size("gy"))).astype(jnp.float32)
+    inside = inside_x[:, None, None] * inside_y[None, :, None]
     pressure = jnp.zeros_like(source)
     for outer_step in range(OUTER):
         if outer_step == 0:
             residual = source
         else:
-            residual = source - neighbour_image(with_halo(pressure, sides, 1), diagonal)[1]
+            residual = source - neighbour_image(widen_faces(pressure), diagonal)[1]
         coarse_rhs = lax.psum(restrict_cells(residual, maps), ("gx", "gy"))
         correction = jnp.dot(coarse_inverse, coarse_rhs * scale_factor, precision=highest)
         pressure = pressure + prolong(correction, maps, source.shape)
-        for _ in range(SWEEPS):
-            pressure = smooth_once(with_halo(pressure, sides, 1), source, diagonal)
+        for _ in range(SWEEPS // 2):
+            widened = with_halo(pressure, (("gx", 0), ("gy", 1)), 2)
+            halfway = (
+                smooth_once(widened, margin[0, 1:-1, 1:-1], margin[1, 1:-1, 1:-1])
+                * inside[1:-1, 1:-1]
+            )
+            pressure = smooth_once(halfway, source, diagonal)
     snapshot = lax.all_to_all(pressure[None], "grp", split_axis=3, concat_axis=0, tiled=True)
     columns = snapshot.reshape(snapshot.shape[0], -1)
     range_flat = range_sketch.reshape(range_sketch.shape[0], -1)

time: 54.4 us -> 54.4 us (level)
  no operation moved by 1% of the time
where the time goes in v2:
time: 54.4 us; the launch traced here: 54.1 us
  starting transfers between devices  17.5 us (32%)
  waiting for transfers between devices  16.8 us (31%)
  blocking collectives  10.2 us (19%)
  Pallas kernels  8.93 us (16%)
  between operations  0.74 us (1%)
    all_to_all x1, blocking collectives, gather(): return lax.all_to_all(copies, axes, 0, 0)  10.2 us
    ppermute x5, starting transfers between devices, fast_body(): others.append(lax.ppermute(sent, ('grp', 'gx', 'gy'), pairs(phase)))  9.58 us
    ppermute x3, waiting for transfers between devices, fast_body(): lax.ppermute(gathered, axis, [(i, i ^ bit) for i in range(count)])  8.37 us
    pallas_call x6, Pallas kernels, call(): pl.pallas_call(kernel, out_shape=shapes, in_specs=specs or [vmem] * len(i...  7.64 us
    all_to_all x1, waiting for transfers between devices, gather(): return lax.all_to_all(copies, axes, 0, 0)  5.7 us
    ppermute x3, starting transfers between devices, fast_body(): lax.ppermute(gathered, axis, [(i, i ^ bit) for i in range(count)])  3.28 us
    all_to_all x1, starting transfers between devices, gather(): return lax.all_to_all(copies, axes, 0, 0)  2.68 us
    ppermute x3, waiting for transfers between devices, fast_body(): lax.ppermute(pieces[turn], 'grp', [(at, at ^ turn) for at in range(groups)])  2.33 us
  transfers between devices with their start and end apart: 12, of which 7 were waited for; matrix products, arithmetic and copies ran while one was open for 0% of the time, Pallas kernels for 4%

profile of v2, /device:TPU:0, one launch (start us, length us, event | category | flops | bytes accessed | tf_op | source)
XLA Modules:
  0.0 54.1 jit_solution(7368100069030364678)
XLA Ops:
  0.6 1.3 %begin.1 = (f32[2,4,8,512]{3,2,1,0:T(8,128)S(1)}, s32[4,8,512]{2,1,0:T(8,128)S(1)}, f32[256,256]{1,0:T(8,128)S(1)}, f32[3,128]{1,0:T(4,128)S(1)}) custom-call(f32[4,8,512]{2,1,0:T(8,128)} %bitcast.4, f32[4,8,512]{2,1,0:T(8,128)} %diagonal_from.1, s32[4,8,512]{2,1,0:T(8,128)} %ids_from.1, f32[256,256]{1,0:T(8,128)} %inverse_from.1), custom_call_target="tpu_custom_call" | custom-call | tf_op jit(solution)/shard_map/begin/pallas_call | solution.py:455
  1.9 3.1 %collective-permute-start = (f32[2,4,8,512]{3,2,1,0:T(8,128)S(1)}, f32[2,4,8,512]{3,2,1,0:T(8,128)S(1)}, u32[]{:S(2)}, u32[]{:S(2)}) collective-permute-start(f32[2,4,8,512]{3,2,1,0:T(8,128)S(1)} %get-tuple-element.17.own_ref), channel_id=1, source_target_pairs={{0,4},{1,5},{2,6},{3,7},{4,0},{5,1},{6,2},{7,3},{8,12},{9,13},{10,... | collective-permute-start | bytes 393224 | tf_op jit(solution)/shard_map/ppermute | solution.py:472
  5.0 0.0 collective-permute-start.3
  5.0 3.1 %collective-permute-start.1 = (f32[2,4,8,512]{3,2,1,0:T(8,128)S(1)}, f32[2,4,8,512]{3,2,1,0:T(8,128)S(1)}, u32[]{:S(2)}, u32[]{:S(2)}) collective-permute-start(f32[2,4,8,512]{3,2,1,0:T(8,128)S(1)} %get-tuple-element.17.own_ref), channel_id=1, source_target_pairs={{0,1},{1,0},{2,3},{3,2},{4,5},{5,4},{6,7},{7,6},{8,9},{9,8},{10,11... | collective-permute-start | bytes 393224 | tf_op jit(solution)/shard_map/ppermute | solution.py:472
  8.1 0.3 collective-permute-done.other_ref
  8.5 0.0 collective-permute-start.4
  8.5 3.4 %collective-permute-start.2 = (f32[2,4,8,512]{3,2,1,0:T(8,128)S(1)}, f32[2,4,8,512]{3,2,1,0:T(8,128)S(1)}, u32[]{:S(2)}, u32[]{:S(2)}) collective-permute-start(f32[2,4,8,512]{3,2,1,0:T(8,128)S(1)} %collective-permute-done.other_ref), channel_id=1, source_target_pairs={{0,1},{1,0},{2,3},{3,2},{4,5},{5,4},{6,7},{7,6},{8,9},{9,8},{10,11... | collective-permute-start | bytes 393224 | tf_op jit(solution)/shard_map/ppermute | solution.py:472
  11.9 1.0 %collective-permute-start.5 = (f32[3,128]{1,0:T(4,128)S(1)}, f32[3,128]{1,0:T(4,128)S(1)}, u32[]{:S(2)}, u32[]{:S(2)}) collective-permute-start(f32[3,128]{1,0:T(4,128)S(1)} %get-tuple-element.20), channel_id=1, source_target_pairs={{0,2},{1,3},{2,0},{3,1},{4,6},{5,7},{6,4},{7,5},{8,10},{9,11},{10,... | collective-permute-start | bytes 4616 | tf_op jit(solution)/shard_map/ppermute | solution.py:478
  12.9 3.5 %collective-permute-done.5 = f32[3,128]{1,0:T(4,128)S(1)} collective-permute-done((f32[3,128]{1,0:T(4,128)S(1)}, f32[3,128]{1,0:T(4,128)S(1)}, u32[]{:S(2)}, u32[]{:S(2)}) %collective-permute-start.5) | collective-permute-done | bytes 1568 | tf_op jit(solution)/shard_map/ppermute | solution.py:478
  16.3 0.7 %collective-permute-start.6 = (f32[3,128]{1,0:T(4,128)S(1)}, f32[3,128]{1,0:T(4,128)S(1)}, u32[]{:S(2)}, u32[]{:S(2)}) collective-permute-start(f32[3,128]{1,0:T(4,128)S(1)} %add.9), channel_id=1, source_target_pairs={{0,1},{1,0},{2,3},{3,2},{4,5},{5,4},{6,7},{7,6},{8,9},{9,8},{10,11... | collective-permute-start | bytes 4616 | tf_op jit(solution)/shard_map/ppermute | solution.py:478
  17.1 2.8 %collective-permute-done.6 = f32[3,128]{1,0:T(4,128)S(1)} collective-permute-done((f32[3,128]{1,0:T(4,128)S(1)}, f32[3,128]{1,0:T(4,128)S(1)}, u32[]{:S(2)}, u32[]{:S(2)}) %collective-permute-start.6) | collective-permute-done | bytes 1568 | tf_op jit(solution)/shard_map/ppermute | solution.py:478
  19.9 1.5 %collective-permute-start.7 = (f32[3,128]{1,0:T(4,128)S(1)}, f32[3,128]{1,0:T(4,128)S(1)}, u32[]{:S(2)}, u32[]{:S(2)}) collective-permute-start(f32[3,128]{1,0:T(4,128)S(1)} %add.10), channel_id=1, source_target_pairs={{0,4},{4,0},{1,5},{5,1},{2,6},{6,2},{3,7},{7,3},{8,12},{12,8},{9,1... | collective-permute-start | bytes 4616 | tf_op jit(solution)/shard_map/ppermute | solution.py:478
  21.5 2.1 %collective-permute-done.7 = f32[3,128]{1,0:T(4,128)S(1)} collective-permute-done((f32[3,128]{1,0:T(4,128)S(1)}, f32[3,128]{1,0:T(4,128)S(1)}, u32[]{:S(2)}, u32[]{:S(2)}) %collective-permute-start.7) | collective-permute-done | bytes 1568 | tf_op jit(solution)/shard_map/ppermute | solution.py:478
  23.5 0.0 collective-permute-done.3.odd_ref
  23.5 0.0 collective-permute-done.1.even_ref
  23.5 0.0 collective-permute-done.4.odd_other_ref
  23.5 0.0 collective-permute-done.2.even_other_ref
  23.6 2.2 %shard_map.121 = (f32[10,24,512]{2,1,0:T(8,128)S(1)}, f32[8,24,512]{2,1,0:T(8,128)S(1)}, f32[8,24,512]{2,1,0:T(8,128)S(1)}, f32[8,3,128]{2,1,0:T(4,128)S(1)}) custom-call(f32[2,4,8,512]{3,2,1,0:T(8,128)S(1)} %get-tuple-element.17.own_ref, f32[2,4,8,512]{3,2,1,0:T(8,128)S(1)} %collective-permute-done.other_ref, ...), custom_call_target="tpu_custom_call" | custom-call | tf_op jit(solution)/shard_map/pallas_call | solution.py:404
  25.7 0.0 copy-start
  25.8 10.2 %all_to_all.10.gathered_ref = f32[8,3,128]{2,1,0:T(4,128)S(1)} all-to-all(f32[8,3,128]{2,1,0:T(4,128)S(1)} %get-tuple-element.24), channel_id=1, replica_groups=mesh['grp'=4,'gx'=2,'gy'=4] {'gx','gy'}, dimensions={0} | all-to-all | bytes 24576 | tf_op jit(solution)/shard_map/all_to_all | solution.py:420
  36.0 0.0 copy-start.1
  36.0 1.3 %shard_map.122 = (f32[4,8,128]{2,1,0:T(8,128)S(1)}, f32[4,8,128]{2,1,0:T(8,128)S(1)}, f32[4,8,128]{2,1,0:T(8,128)S(1)}, f32[4,8,128]{2,1,0:T(8,128)S(1)}) custom-call(f32[10,24,512]{2,1,0:T(8,128)S(1)} %get-tuple-element.21.field_ref, f32[8,24,512]{2,1,0:T(8,128)S(1)} %get-tuple-element.22.weight_ref, f32[8,24,512]{2,1,0:T(8,128)S(1)} %get-tuple-element.23.drive_ref, ...), custom_call_target="tpu_custom_call" | custom-call | tf_op jit(solution)/shard_map/pallas_call | solution.py:404
  37.2 0.1 collective-permute-start.8
  37.3 1.6 %collective-permute-start.9 = (f32[4,8,128]{2,1,0:T(8,128)S(1)}, f32[4,8,128]{2,1,0:T(8,128)S(1)}, u32[]{:S(2)}, u32[]{:S(2)}) collective-permute-start(f32[4,8,128]{2,1,0:T(8,128)S(1)} %get-tuple-element.27), channel_id=1, source_target_pairs={{0,16},{8,24},{16,0},{24,8},{1,17},{9,25},{17,1},{25,9},{2,18},{10... | collective-permute-start | bytes 49160 | tf_op jit(solution)/shard_map/ppermute | solution.py:494
  38.9 0.3 collective-permute-start.10
  39.2 0.0 collective-permute-done.8.rest_1_
  39.2 0.0 copy-done
  39.2 0.0 copy-done.1
  39.2 0.5 shard_map.124.early_ref
  39.7 0.0 copy-start.2
  39.7 1.4 %collective-permute-done.9.rest_2_.rest_0_ = f32[4,8,128]{2,1,0:T(8,128)S(1)} collective-permute-done((f32[4,8,128]{2,1,0:T(8,128)S(1)}, f32[4,8,128]{2,1,0:T(8,128)S(1)}, u32[]{:S(2)}, u32[]{:S(2)}) %collective-permute-start.9) | collective-permute-done | bytes 16416 | tf_op jit(solution)/shard_map/ppermute | solution.py:494
  41.1 0.9 %collective-permute-done.10.rest_3_.rest_1_ = f32[4,8,128]{2,1,0:T(8,128)S(1)} collective-permute-done((f32[4,8,128]{2,1,0:T(8,128)S(1)}, f32[4,8,128]{2,1,0:T(8,128)S(1)}, u32[]{:S(2)}, u32[]{:S(2)}) %collective-permute-start.10) | collective-permute-done | bytes 16416 | tf_op jit(solution)/shard_map/ppermute | solution.py:494
  42.0 1.2 %shard_map.125 = f32[32,4,128]{2,1,0:T(4,128)} custom-call(f32[32,4,8,128]{3,2,1,0:T(8,128)S(1)} %copy-done.1, f32[64,4,8,128]{3,2,1,0:T(8,128)S(1)} %copy-done, f32[2,128]{1,0:T(2,128)S(1)} %shard_map.124.early_ref, f32[4,8,128]{2,1,0:T(8,128)S(1)} %collective-permute-done.9.rest_2_.rest_0_, f32[4,8,128]{2,1,0:T(8,128)S(1)} %collective-permute-done.10.rest_3_.rest_1_), custom_call_target="tpu_custom_call" | custom-call | tf_op jit(solution)/shard_map/pallas_call | solution.py:404
  43.2 0.0 copy-start.4
  43.2 2.7 %all-to-all-start.1 = ((f32[32,4,128]{2,1,0:T(4,128)}), f32[32,4,128]{2,1,0:T(4,128)S(1)}, u32[]{:S(2)}, u32[]{:S(2)}) async-start(f32[32,4,128]{2,1,0:T(4,128)} %shard_map.125), calls=%async_computation.1 | async-start | bytes 131072 | tf_op jit(solution)/shard_map/all_to_all | solution.py:420
  45.9 0.0 copy-done.2
  45.9 0.0 copy-done.4
  45.9 0.0 copy-start.3
  45.9 0.0 copy-start.5
  46.0 1.5 %shard_map.123 = f32[32,4,8,128]{3,2,1,0:T(8,128)} custom-call(f32[4,32]{1,0:T(4,128)S(1)} %copy-done.4, f32[32,4,8,128]{3,2,1,0:T(8,128)S(1)} %copy-done.2, f32[4,8,128]{2,1,0:T(8,128)S(1)} %get-tuple-element.25.rest_0_, f32[4,8,128]{2,1,0:T(8,128)S(1)} %collective-permute-done.8.rest_1_, f32[4,8,128]{2,1,0:T(8,128)S(1)} %collective-permute-done.9.rest_2_.rest_0_, ...), custom_call_target="tpu_custom_call" | custom-call | tf_op jit(solution)/shard_map/pallas_call | solution.py:404
  47.5 5.7 %all-to-all-done.1.gathered_ref = f32[32,4,128]{2,1,0:T(4,128)S(1)} async-done(((f32[32,4,128]{2,1,0:T(4,128)}), f32[32,4,128]{2,1,0:T(4,128)S(1)}, u32[]{:S(2)}, u32[]{:S(2)}) %all-to-all-start.1) | async-done | bytes 65568 | tf_op jit(solution)/shard_map/all_to_all | solution.py:420
  53.2 0.0 copy-done.3
  53.2 0.0 copy-done.5
  53.2 0.9 %shard_map.126 = (f32[4,32]{1,0:T(4,128)}, f32[64,64]{1,0:T(8,128)}) custom-call(f32[32,4,128]{2,1,0:T(4,128)S(1)} %all-to-all-done.1.gathered_ref, f32[4,64]{1,0:T(4,128)S(1)} %bitcast.3, f32[64,64]{1,0:T(8,128)S(1)} %copy-done.3), custom_call_target="tpu_custom_call" | custom-call | tf_op jit(solution)/shard_map/pallas_call | solution.py:404
  (3 shorter events, 0.0 us)
Async XLA Ops:
  1.9 6.6 %collective-permute-start = (f32[2,4,8,512]{3,2,1,0:T(8,128)S(1)}, f32[2,4,8,512]{3,2,1,0:T(8,128)S(1)}, u32[]{:S(2)}, u32[]{:S(2)}) collective-permute-start(f32[2,4,8,512]{3,2,1,0:T(8,128)S(1)} %get-tuple-element.17.own_ref), channel_id=1, source_target_pairs={{0,4},{1,5},{2,6},{3,7},{4,0},{5,1},{6,2},{7,3},{8,12},{9,13},{10,... | collective-permute-start | bytes 393224 | tf_op jit(solution)/shard_map/ppermute | solution.py:472
  5.0 18.5 %collective-permute-start.3 = (f32[2,4,8,512]{3,2,1,0:T(8,128)S(1)}, f32[2,4,8,512]{3,2,1,0:T(8,128)S(1)}, u32[]{:S(2)}, u32[]{:S(2)}) collective-permute-start(f32[2,4,8,512]{3,2,1,0:T(8,128)S(1)} %get-tuple-element.17.own_ref), channel_id=1, source_target_pairs={{0,8},{1,2},{2,1},{3,11},{4,12},{5,6},{6,5},{7,15},{8,0},{9,10},{1... | collective-permute-start | bytes 393224 | tf_op jit(solution)/shard_map/ppermute | solution.py:472
  5.0 18.5 %collective-permute-start.1 = (f32[2,4,8,512]{3,2,1,0:T(8,128)S(1)}, f32[2,4,8,512]{3,2,1,0:T(8,128)S(1)}, u32[]{:S(2)}, u32[]{:S(2)}) collective-permute-start(f32[2,4,8,512]{3,2,1,0:T(8,128)S(1)} %get-tuple-element.17.own_ref), channel_id=1, source_target_pairs={{0,1},{1,0},{2,3},{3,2},{4,5},{5,4},{6,7},{7,6},{8,9},{9,8},{10,11... | collective-permute-start | bytes 393224 | tf_op jit(solution)/shard_map/ppermute | solution.py:472
  8.5 15.1 %collective-permute-start.4 = (f32[2,4,8,512]{3,2,1,0:T(8,128)S(1)}, f32[2,4,8,512]{3,2,1,0:T(8,128)S(1)}, u32[]{:S(2)}, u32[]{:S(2)}) collective-permute-start(f32[2,4,8,512]{3,2,1,0:T(8,128)S(1)} %collective-permute-done.other_ref), channel_id=1, source_target_pairs={{0,8},{1,2},{2,1},{3,11},{4,12},{5,6},{6,5},{7,15},{8,0},{9,10},{1... | collective-permute-start | bytes 393224 | tf_op jit(solution)/shard_map/ppermute | solution.py:472
  8.5 15.1 %collective-permute-start.2 = (f32[2,4,8,512]{3,2,1,0:T(8,128)S(1)}, f32[2,4,8,512]{3,2,1,0:T(8,128)S(1)}, u32[]{:S(2)}, u32[]{:S(2)}) collective-permute-start(f32[2,4,8,512]{3,2,1,0:T(8,128)S(1)} %collective-permute-done.other_ref), channel_id=1, source_target_pairs={{0,1},{1,0},{2,3},{3,2},{4,5},{5,4},{6,7},{7,6},{8,9},{9,8},{10,11... | collective-permute-start | bytes 393224 | tf_op jit(solution)/shard_map/ppermute | solution.py:472
  11.9 4.5 %collective-permute-start.5 = (f32[3,128]{1,0:T(4,128)S(1)}, f32[3,128]{1,0:T(4,128)S(1)}, u32[]{:S(2)}, u32[]{:S(2)}) collective-permute-start(f32[3,128]{1,0:T(4,128)S(1)} %get-tuple-element.20), channel_id=1, source_target_pairs={{0,2},{1,3},{2,0},{3,1},{4,6},{5,7},{6,4},{7,5},{8,10},{9,11},{10,... | collective-permute-start | bytes 4616 | tf_op jit(solution)/shard_map/ppermute | solution.py:478
  16.3 3.6 %collective-permute-start.6 = (f32[3,128]{1,0:T(4,128)S(1)}, f32[3,128]{1,0:T(4,128)S(1)}, u32[]{:S(2)}, u32[]{:S(2)}) collective-permute-start(f32[3,128]{1,0:T(4,128)S(1)} %add.9), channel_id=1, source_target_pairs={{0,1},{1,0},{2,3},{3,2},{4,5},{5,4},{6,7},{7,6},{8,9},{9,8},{10,11... | collective-permute-start | bytes 4616 | tf_op jit(solution)/shard_map/ppermute | solution.py:478
  19.9 3.6 %collective-permute-start.7 = (f32[3,128]{1,0:T(4,128)S(1)}, f32[3,128]{1,0:T(4,128)S(1)}, u32[]{:S(2)}, u32[]{:S(2)}) collective-permute-start(f32[3,128]{1,0:T(4,128)S(1)} %add.10), channel_id=1, source_target_pairs={{0,4},{4,0},{1,5},{5,1},{2,6},{6,2},{3,7},{7,3},{8,12},{12,8},{9,1... | collective-permute-start | bytes 4616 | tf_op jit(solution)/shard_map/ppermute | solution.py:478
  25.7 13.4 %copy-start = (f32[64,4,8,128]{3,2,1,0:T(8,128)S(1)}, f32[64,4,8,128]{3,2,1,0:T(8,128)}, u32[]{:S(2)}) copy-start(f32[64,4,8,128]{3,2,1,0:T(8,128)} %phi_ref.3) | copy-start | bytes 3145732
  36.0 3.2 %copy-start.1 = (f32[32,4,8,128]{3,2,1,0:T(8,128)S(1)}, f32[32,4,8,128]{3,2,1,0:T(8,128)}, u32[]{:S(2)}) copy-start(f32[32,4,8,128]{3,2,1,0:T(8,128)} %psi_ref.3) | copy-start | bytes 1572868
  37.2 1.9 %collective-permute-start.8 = (f32[4,8,128]{2,1,0:T(8,128)S(1)}, f32[4,8,128]{2,1,0:T(8,128)S(1)}, u32[]{:S(2)}, u32[]{:S(2)}) collective-permute-start(f32[4,8,128]{2,1,0:T(8,128)S(1)} %get-tuple-element.26), channel_id=1, source_target_pairs={{0,8},{8,0},{16,24},{24,16},{1,9},{9,1},{17,25},{25,17},{2,10},{10... | collective-permute-start | bytes 49160 | tf_op jit(solution)/shard_map/ppermute | solution.py:494
  37.3 3.8 %collective-permute-start.9 = (f32[4,8,128]{2,1,0:T(8,128)S(1)}, f32[4,8,128]{2,1,0:T(8,128)S(1)}, u32[]{:S(2)}, u32[]{:S(2)}) collective-permute-start(f32[4,8,128]{2,1,0:T(8,128)S(1)} %get-tuple-element.27), channel_id=1, source_target_pairs={{0,16},{8,24},{16,0},{24,8},{1,17},{9,25},{17,1},{25,9},{2,18},{10... | collective-permute-start | bytes 49160 | tf_op jit(solution)/shard_map/ppermute | solution.py:494
  38.9 3.2 %collective-permute-start.10 = (f32[4,8,128]{2,1,0:T(8,128)S(1)}, f32[4,8,128]{2,1,0:T(8,128)S(1)}, u32[]{:S(2)}, u32[]{:S(2)}) collective-permute-start(f32[4,8,128]{2,1,0:T(8,128)S(1)} %get-tuple-element.28), channel_id=1, source_target_pairs={{0,24},{8,16},{16,8},{24,0},{1,25},{9,17},{17,9},{25,1},{2,26},{10... | collective-permute-start | bytes 49160 | tf_op jit(solution)/shard_map/ppermute | solution.py:494
  39.7 6.2 %copy-start.2 = (f32[32,4,8,128]{3,2,1,0:T(8,128)S(1)}, f32[32,4,8,128]{3,2,1,0:T(8,128)}, u32[]{:S(2)}) copy-start(f32[32,4,8,128]{3,2,1,0:T(8,128)} %range_ref.1) | copy-start | bytes 1572868
  43.2 2.7 %copy-start.4 = (f32[4,32]{1,0:T(4,128)S(1)}, f32[4,32]{1,0:T(4,128)}, u32[]{:S(2)}) copy-start(f32[4,32]{1,0:T(4,128)} %omega_ref.1) | copy-start | bytes 1540
  43.2 10.0 %all-to-all-start.1 = ((f32[32,4,128]{2,1,0:T(4,128)}), f32[32,4,128]{2,1,0:T(4,128)S(1)}, u32[]{:S(2)}, u32[]{:S(2)}) async-start(f32[32,4,128]{2,1,0:T(4,128)} %shard_map.125), calls=%async_computation.1 | async-start | bytes 131072 | tf_op jit(solution)/shard_map/all_to_all | solution.py:420
  45.9 7.3 %copy-start.3 = (f32[64,64]{1,0:T(8,128)S(1)}, f32[64,64]{1,0:T(8,128)}, u32[]{:S(2)}) copy-start(f32[64,64]{1,0:T(8,128)} %core_ref.1) | copy-start | bytes 49156
  45.9 7.2 %copy-start.5 = (f32[64,4]{0,1:T(4,128)S(1)}, f32[64,4]{0,1:T(4,128)}, u32[]{:S(2)}) copy-start(f32[64,4]{0,1:T(4,128)} %param.17) | copy-start | bytes 3076

commit v3 on v2

--- a/solution.py
+++ b/solution.py
@@ -228,32 +228,51 @@
     field_ref[window_x + 1] = empty
 
 
+def fill(blocks, weight_ref, drive_ref):
+    for ref, first, row, scale in blocks:
+        _, rows_x, rows_y, _ = ref.shape
+        for at in range(rows_x):
+            plane = mirrored(at, rows_x - 1)
+            weight = scale / (6.0 + ref[1, plane])
+            weight_ref[first + at, pl.ds(row, rows_y), :] = weight
+            drive_ref[first + at, pl.ds(row, rows_y), :] = weight * ref[0, plane]
+
+
+def pair_places(count_y, rows_y):
+    at_y = lax.axis_index("gy")
+    parity = lax.rem(at_y, 2)
+    even_row = pl.multiple_of((1 - parity) * 2 * rows_y, SUBLANES)
+    odd_row = pl.multiple_of(parity * 2 * rows_y, SUBLANES)
+    odd_inside = jnp.where((at_y > 0) & (at_y < count_y - 1), jacobi_weight, 0.0)
+    return even_row, odd_row, odd_inside
+
+
+def prepare_kernel(count_y, own_ref, other_ref, even_ref, odd_ref, weight_ref, drive_ref):
+    _, rows_x, rows_y, _ = own_ref.shape
+    even_row, odd_row, odd_inside = pair_places(count_y, rows_y)
+    blocks = (
+        (own_ref, 0, rows_y, jacobi_weight),
+        (other_ref, rows_x, rows_y, jacobi_weight),
+        (even_ref, 0, even_row, jacobi_weight),
+        (odd_ref, 0, odd_row, odd_inside),
+    )
+    fill(blocks, weight_ref, drive_ref)
+
+
 def first_kernel(
-    counts, scale_factor, own_ref, other_ref, even_ref, even_other_ref, odd_ref, odd_other_ref,
-    ids_ref, inverse_ref, gathered_ref,
+    counts, scale_factor, own_ref, even_other_ref, odd_other_ref, ids_ref, inverse_ref,
+    gathered_ref, weight_from, drive_from,
     field_ref, weight_ref, drive_ref, out_ref, spare_ref,
 ):
     count_x, count_y = counts
     _, rows_x, rows_y, cells_z = own_ref.shape
     window_x, window_y, _ = weight_ref.shape
-    at_y = lax.axis_index("gy")
-    parity = lax.rem(at_y, 2)
-    even_row = pl.multiple_of((1 - parity) * 2 * rows_y, SUBLANES)
-    odd_row = pl.multiple_of(parity * 2 * rows_y, SUBLANES)
-    odd_inside = jnp.where((at_y > 0) & (at_y < count_y - 1), jacobi_weight, 0.0)
-    for ref, first, row, scale in (
-        (own_ref, 0, rows_y, jacobi_weight),
-        (other_ref, rows_x, rows_y, jacobi_weight),
-        (even_ref, 0, even_row, jacobi_weight),
+    even_row, odd_row, odd_inside = pair_places(count_y, rows_y)
+    blocks = (
         (even_other_ref, rows_x, even_row, jacobi_weight),
-        (odd_ref, 0, odd_row, odd_inside),
         (odd_other_ref, rows_x, odd_row, odd_inside),
-    ):
-        for at in range(rows_x):
-            plane = mirrored(at, rows_x - 1)
-            weight = scale / (6.0 + ref[1, plane])
-            weight_ref[first + at, pl.ds(row, rows_y), :] = weight
-            drive_ref[first + at, pl.ds(row, rows_y), :] = weight * ref[0, plane]
+    )
+    fill(blocks, weight_ref, drive_ref)
 
     parts = inverse_ref.shape[0] // LANES
     rows = [gathered_ref[at : at + 1] for at in range(parts + 1)]
@@ -398,7 +417,7 @@
 smem = pl.BlockSpec(memory_space=pltpu.SMEM)
 
 
-def call(kernel, outs, inputs, scratch=(), specs=None):
+def call(kernel, outs, inputs, scratch=(), specs=None, aliases=None):
     many = isinstance(outs, list)
     shapes = [jax.ShapeDtypeStruct(shape, jnp.float32) for shape in (outs if many else [outs])]
     result = pl.pallas_call(
@@ -408,6 +427,7 @@
         out_specs=[vmem] * len(shapes),
         scratch_shapes=[pltpu.VMEM(shape, jnp.float32) for shape in scratch],
         compiler_params=pltpu.CompilerParams(vmem_limit_bytes=VMEM_BYTES),
+        input_output_aliases=aliases or {},
     )(*inputs)
     return result if many else result[0]
 
@@ -476,11 +496,17 @@
     turns.append(("gx", count_x, 1))
     for axis, count, bit in turns:
         gathered = gathered + lax.ppermute(gathered, axis, [(i, i ^ bit) for i in range(count)])
+    prepared = call(
+        functools.partial(prepare_kernel, count_y),
+        [window, window],
+        (mine, others[0], others[1], others[3]),
+    )
     field, weight, drive, partial = call(
         functools.partial(first_kernel, counts, scale_factor),
         [padded, window, window, copies],
-        (mine, *others, ids, inverse, gathered),
+        (mine, others[2], others[4], ids, inverse, gathered, *prepared),
         scratch=[padded],
+        aliases={6: 1, 7: 2},
     )
     gathered = gather(partial, ("gx", "gy"))
     chunk = cells_z // groups

time: 54.4 us -> 54.3 us (level)
    pallas_call x6 -> x7, Pallas kernels: 7.64 us -> 7.58 us  [call(): pl.pallas_call(kernel, out_shape=shapes, in_specs=specs or [vmem] * len(i...]
where the time goes in v3:
time: 54.3 us; the launch traced here: 54.1 us
  starting transfers between devices  17.5 us (32%)
  waiting for transfers between devices  16.8 us (31%)
  blocking collectives  10.2 us (19%)
  Pallas kernels  8.87 us (16%)
  between operations  0.75 us (1%)
    all_to_all x1, blocking collectives, gather(): return lax.all_to_all(copies, axes, 0, 0)  10.2 us
    ppermute x5, starting transfers between devices, fast_body(): others.append(lax.ppermute(sent, ('grp', 'gx', 'gy'), pairs(phase)))  9.58 us
    ppermute x3, waiting for transfers between devices, fast_body(): lax.ppermute(gathered, axis, [(i, i ^ bit) for i in range(count)])  8.37 us
    pallas_call x7, Pallas kernels, call(): pl.pallas_call(kernel, out_shape=shapes, in_specs=specs or [vmem] * len(i...  7.58 us
    all_to_all x1, waiting for transfers between devices, gather(): return lax.all_to_all(copies, axes, 0, 0)  5.7 us
    ppermute x3, starting transfers between devices, fast_body(): lax.ppermute(gathered, axis, [(i, i ^ bit) for i in range(count)])  3.28 us
    all_to_all x1, starting transfers between devices, gather(): return lax.all_to_all(copies, axes, 0, 0)  2.68 us
    ppermute x3, waiting for transfers between devices, fast_body(): lax.ppermute(pieces[turn], 'grp', [(at, at ^ turn) for at in range(groups)])  2.33 us
  transfers between devices with their start and end apart: 12, of which 7 were waited for; matrix products, arithmetic and copies ran while one was open for 0% of the time, Pallas kernels for 4%

profile of v3, /device:TPU:0, one launch (start us, length us, event | category | flops | bytes accessed | tf_op | source)
XLA Modules:
  0.0 54.1 jit_solution(3227480122248132956)
XLA Ops:
  0.6 1.3 %begin.1 = (f32[2,4,8,512]{3,2,1,0:T(8,128)S(1)}, s32[4,8,512]{2,1,0:T(8,128)S(1)}, f32[256,256]{1,0:T(8,128)S(1)}, f32[3,128]{1,0:T(4,128)S(1)}) custom-call(f32[4,8,512]{2,1,0:T(8,128)} %bitcast.4, f32[4,8,512]{2,1,0:T(8,128)} %diagonal_from.1, s32[4,8,512]{2,1,0:T(8,128)} %ids_from.1, f32[256,256]{1,0:T(8,128)} %inverse_from.1), custom_call_target="tpu_custom_call" | custom-call | tf_op jit(solution)/shard_map/begin/pallas_call | solution.py:475
  1.9 3.1 %collective-permute-start = (f32[2,4,8,512]{3,2,1,0:T(8,128)S(1)}, f32[2,4,8,512]{3,2,1,0:T(8,128)S(1)}, u32[]{:S(2)}, u32[]{:S(2)}) collective-permute-start(f32[2,4,8,512]{3,2,1,0:T(8,128)S(1)} %get-tuple-element.19.own_ref), channel_id=1, source_target_pairs={{0,4},{1,5},{2,6},{3,7},{4,0},{5,1},{6,2},{7,3},{8,12},{9,13},{10,... | collective-permute-start | bytes 393224 | tf_op jit(solution)/shard_map/ppermute | solution.py:492
  5.0 0.0 collective-permute-start.7
  5.0 3.1 %collective-permute-start.6 = (f32[2,4,8,512]{3,2,1,0:T(8,128)S(1)}, f32[2,4,8,512]{3,2,1,0:T(8,128)S(1)}, u32[]{:S(2)}, u32[]{:S(2)}) collective-permute-start(f32[2,4,8,512]{3,2,1,0:T(8,128)S(1)} %get-tuple-element.19.own_ref), channel_id=1, source_target_pairs={{0,1},{1,0},{2,3},{3,2},{4,5},{5,4},{6,7},{7,6},{8,9},{9,8},{10,11... | collective-permute-start | bytes 393224 | tf_op jit(solution)/shard_map/ppermute | solution.py:492
  8.1 0.3 collective-permute-done.other_ref
  8.5 0.0 collective-permute-start.2
  8.5 3.4 %collective-permute-start.1 = (f32[2,4,8,512]{3,2,1,0:T(8,128)S(1)}, f32[2,4,8,512]{3,2,1,0:T(8,128)S(1)}, u32[]{:S(2)}, u32[]{:S(2)}) collective-permute-start(f32[2,4,8,512]{3,2,1,0:T(8,128)S(1)} %collective-permute-done.other_ref), channel_id=1, source_target_pairs={{0,1},{1,0},{2,3},{3,2},{4,5},{5,4},{6,7},{7,6},{8,9},{9,8},{10,11... | collective-permute-start | bytes 393224 | tf_op jit(solution)/shard_map/ppermute | solution.py:492
  11.9 1.0 %collective-permute-start.3 = (f32[3,128]{1,0:T(4,128)S(1)}, f32[3,128]{1,0:T(4,128)S(1)}, u32[]{:S(2)}, u32[]{:S(2)}) collective-permute-start(f32[3,128]{1,0:T(4,128)S(1)} %get-tuple-element.22), channel_id=1, source_target_pairs={{0,2},{1,3},{2,0},{3,1},{4,6},{5,7},{6,4},{7,5},{8,10},{9,11},{10,... | collective-permute-start | bytes 4616 | tf_op jit(solution)/shard_map/ppermute | solution.py:498
  12.9 3.5 %collective-permute-done.3 = f32[3,128]{1,0:T(4,128)S(1)} collective-permute-done((f32[3,128]{1,0:T(4,128)S(1)}, f32[3,128]{1,0:T(4,128)S(1)}, u32[]{:S(2)}, u32[]{:S(2)}) %collective-permute-start.3) | collective-permute-done | bytes 1568 | tf_op jit(solution)/shard_map/ppermute | solution.py:498
  16.3 0.7 %collective-permute-start.4 = (f32[3,128]{1,0:T(4,128)S(1)}, f32[3,128]{1,0:T(4,128)S(1)}, u32[]{:S(2)}, u32[]{:S(2)}) collective-permute-start(f32[3,128]{1,0:T(4,128)S(1)} %add.9), channel_id=1, source_target_pairs={{0,1},{1,0},{2,3},{3,2},{4,5},{5,4},{6,7},{7,6},{8,9},{9,8},{10,11... | collective-permute-start | bytes 4616 | tf_op jit(solution)/shard_map/ppermute | solution.py:498
  17.1 2.8 %collective-permute-done.4 = f32[3,128]{1,0:T(4,128)S(1)} collective-permute-done((f32[3,128]{1,0:T(4,128)S(1)}, f32[3,128]{1,0:T(4,128)S(1)}, u32[]{:S(2)}, u32[]{:S(2)}) %collective-permute-start.4) | collective-permute-done | bytes 1568 | tf_op jit(solution)/shard_map/ppermute | solution.py:498
  19.9 1.5 %collective-permute-start.5 = (f32[3,128]{1,0:T(4,128)S(1)}, f32[3,128]{1,0:T(4,128)S(1)}, u32[]{:S(2)}, u32[]{:S(2)}) collective-permute-start(f32[3,128]{1,0:T(4,128)S(1)} %add.10), channel_id=1, source_target_pairs={{0,4},{4,0},{1,5},{5,1},{2,6},{6,2},{3,7},{7,3},{8,12},{12,8},{9,1... | collective-permute-start | bytes 4616 | tf_op jit(solution)/shard_map/ppermute | solution.py:498
  21.5 2.1 %collective-permute-done.5 = f32[3,128]{1,0:T(4,128)S(1)} collective-permute-done((f32[3,128]{1,0:T(4,128)S(1)}, f32[3,128]{1,0:T(4,128)S(1)}, u32[]{:S(2)}, u32[]{:S(2)}) %collective-permute-start.5) | collective-permute-done | bytes 1568 | tf_op jit(solution)/shard_map/ppermute | solution.py:498
  23.5 0.0 collective-permute-done.7.odd_ref
  23.5 0.0 collective-permute-done.6.even_ref
  23.5 0.1 shard_map.121
  23.6 0.0 collective-permute-done.2.odd_other_ref
  23.6 0.0 collective-permute-done.1.even_other_ref
  23.6 2.1 %shard_map.122 = (f32[10,24,512]{2,1,0:T(8,128)S(1)}, f32[8,24,512]{2,1,0:T(8,128)S(1)}, f32[8,24,512]{2,1,0:T(8,128)S(1)}, f32[8,3,128]{2,1,0:T(4,128)S(1)}) custom-call(f32[2,4,8,512]{3,2,1,0:T(8,128)S(1)} %get-tuple-element.19.own_ref, f32[2,4,8,512]{3,2,1,0:T(8,128)S(1)} %collective-permute-done.1.even_other_ref, ...), custom_call_target="tpu_custom_call", output_to_operand_aliasing={{1}: (6, {}), {2}: (7, {})} | custom-call | tf_op jit(solution)/shard_map/pallas_call | solution.py:423
  25.7 0.0 copy-start
  25.8 10.2 %all_to_all.10.gathered_ref = f32[8,3,128]{2,1,0:T(4,128)S(1)} all-to-all(f32[8,3,128]{2,1,0:T(4,128)S(1)} %get-tuple-element.28), channel_id=1, replica_groups=mesh['grp'=4,'gx'=2,'gy'=4] {'gx','gy'}, dimensions={0} | all-to-all | bytes 24576 | tf_op jit(solution)/shard_map/all_to_all | solution.py:440
  36.0 0.0 copy-start.1
  36.0 1.2 %shard_map.123 = (f32[4,8,128]{2,1,0:T(8,128)S(1)}, f32[4,8,128]{2,1,0:T(8,128)S(1)}, f32[4,8,128]{2,1,0:T(8,128)S(1)}, f32[4,8,128]{2,1,0:T(8,128)S(1)}) custom-call(f32[10,24,512]{2,1,0:T(8,128)S(1)} %get-tuple-element.25.field_ref, f32[8,24,512]{2,1,0:T(8,128)S(1)} %get-tuple-element.26.weight_ref, f32[8,24,512]{2,1,0:T(8,128)S(1)} %get-tuple-element.27.drive_ref, ...), custom_call_target="tpu_custom_call" | custom-call | tf_op jit(solution)/shard_map/pallas_call | solution.py:423
  37.2 0.1 collective-permute-start.8
  37.3 1.6 %collective-permute-start.9 = (f32[4,8,128]{2,1,0:T(8,128)S(1)}, f32[4,8,128]{2,1,0:T(8,128)S(1)}, u32[]{:S(2)}, u32[]{:S(2)}) collective-permute-start(f32[4,8,128]{2,1,0:T(8,128)S(1)} %get-tuple-element.31), channel_id=1, source_target_pairs={{0,16},{8,24},{16,0},{24,8},{1,17},{9,25},{17,1},{25,9},{2,18},{10... | collective-permute-start | bytes 49160 | tf_op jit(solution)/shard_map/ppermute | solution.py:520
  38.8 0.3 collective-permute-start.10
  39.1 0.0 collective-permute-done.8.rest_1_
  39.1 0.0 copy-done
  39.1 0.0 copy-done.1
  39.1 0.5 shard_map.125.early_ref
  39.7 0.0 copy-start.2
  39.7 1.4 %collective-permute-done.9.rest_2_.rest_0_ = f32[4,8,128]{2,1,0:T(8,128)S(1)} collective-permute-done((f32[4,8,128]{2,1,0:T(8,128)S(1)}, f32[4,8,128]{2,1,0:T(8,128)S(1)}, u32[]{:S(2)}, u32[]{:S(2)}) %collective-permute-start.9) | collective-permute-done | bytes 16416 | tf_op jit(solution)/shard_map/ppermute | solution.py:520
  41.1 0.9 %collective-permute-done.10.rest_3_.rest_1_ = f32[4,8,128]{2,1,0:T(8,128)S(1)} collective-permute-done((f32[4,8,128]{2,1,0:T(8,128)S(1)}, f32[4,8,128]{2,1,0:T(8,128)S(1)}, u32[]{:S(2)}, u32[]{:S(2)}) %collective-permute-start.10) | collective-permute-done | bytes 16416 | tf_op jit(solution)/shard_map/ppermute | solution.py:520
  42.0 1.2 %shard_map.126 = f32[32,4,128]{2,1,0:T(4,128)} custom-call(f32[32,4,8,128]{3,2,1,0:T(8,128)S(1)} %copy-done.1, f32[64,4,8,128]{3,2,1,0:T(8,128)S(1)} %copy-done, f32[2,128]{1,0:T(2,128)S(1)} %shard_map.125.early_ref, f32[4,8,128]{2,1,0:T(8,128)S(1)} %collective-permute-done.9.rest_2_.rest_0_, f32[4,8,128]{2,1,0:T(8,128)S(1)} %collective-permute-done.10.rest_3_.rest_1_), custom_call_target="tpu_custom_call" | custom-call | tf_op jit(solution)/shard_map/pallas_call | solution.py:423
  43.2 0.0 copy-start.4
  43.2 2.7 %all-to-all-start.1 = ((f32[32,4,128]{2,1,0:T(4,128)}), f32[32,4,128]{2,1,0:T(4,128)S(1)}, u32[]{:S(2)}, u32[]{:S(2)}) async-start(f32[32,4,128]{2,1,0:T(4,128)} %shard_map.126), calls=%async_computation.1 | async-start | bytes 131072 | tf_op jit(solution)/shard_map/all_to_all | solution.py:440
  45.9 0.0 copy-done.2
  45.9 0.0 copy-done.4
  45.9 0.0 copy-start.3
  45.9 0.0 copy-start.5
  45.9 1.5 %shard_map.124 = f32[32,4,8,128]{3,2,1,0:T(8,128)} custom-call(f32[4,32]{1,0:T(4,128)S(1)} %copy-done.4, f32[32,4,8,128]{3,2,1,0:T(8,128)S(1)} %copy-done.2, f32[4,8,128]{2,1,0:T(8,128)S(1)} %get-tuple-element.29.rest_0_, f32[4,8,128]{2,1,0:T(8,128)S(1)} %collective-permute-done.8.rest_1_, f32[4,8,128]{2,1,0:T(8,128)S(1)} %collective-permute-done.9.rest_2_.rest_0_, ...), custom_call_target="tpu_custom_call" | custom-call | tf_op jit(solution)/shard_map/pallas_call | solution.py:423
  47.4 5.7 %all-to-all-done.1.gathered_ref = f32[32,4,128]{2,1,0:T(4,128)S(1)} async-done(((f32[32,4,128]{2,1,0:T(4,128)}), f32[32,4,128]{2,1,0:T(4,128)S(1)}, u32[]{:S(2)}, u32[]{:S(2)}) %all-to-all-start.1) | async-done | bytes 65568 | tf_op jit(solution)/shard_map/all_to_all | solution.py:440
  53.1 0.0 copy-done.3
  53.1 0.0 copy-done.5
  53.1 0.9 %shard_map.127 = (f32[4,32]{1,0:T(4,128)}, f32[64,64]{1,0:T(8,128)}) custom-call(f32[32,4,128]{2,1,0:T(4,128)S(1)} %all-to-all-done.1.gathered_ref, f32[4,64]{1,0:T(4,128)S(1)} %bitcast.3, f32[64,64]{1,0:T(8,128)S(1)} %copy-done.3), custom_call_target="tpu_custom_call" | custom-call | tf_op jit(solution)/shard_map/pallas_call | solution.py:423
  (3 shorter events, 0.0 us)
Async XLA Ops:
  1.9 6.6 %collective-permute-start = (f32[2,4,8,512]{3,2,1,0:T(8,128)S(1)}, f32[2,4,8,512]{3,2,1,0:T(8,128)S(1)}, u32[]{:S(2)}, u32[]{:S(2)}) collective-permute-start(f32[2,4,8,512]{3,2,1,0:T(8,128)S(1)} %get-tuple-element.19.own_ref), channel_id=1, source_target_pairs={{0,4},{1,5},{2,6},{3,7},{4,0},{5,1},{6,2},{7,3},{8,12},{9,13},{10,... | collective-permute-start | bytes 393224 | tf_op jit(solution)/shard_map/ppermute | solution.py:492
  5.0 18.5 %collective-permute-start.7 = (f32[2,4,8,512]{3,2,1,0:T(8,128)S(1)}, f32[2,4,8,512]{3,2,1,0:T(8,128)S(1)}, u32[]{:S(2)}, u32[]{:S(2)}) collective-permute-start(f32[2,4,8,512]{3,2,1,0:T(8,128)S(1)} %get-tuple-element.19.own_ref), channel_id=1, source_target_pairs={{0,8},{1,2},{2,1},{3,11},{4,12},{5,6},{6,5},{7,15},{8,0},{9,10},{1... | collective-permute-start | bytes 393224 | tf_op jit(solution)/shard_map/ppermute | solution.py:492
  5.0 18.5 %collective-permute-start.6 = (f32[2,4,8,512]{3,2,1,0:T(8,128)S(1)}, f32[2,4,8,512]{3,2,1,0:T(8,128)S(1)}, u32[]{:S(2)}, u32[]{:S(2)}) collective-permute-start(f32[2,4,8,512]{3,2,1,0:T(8,128)S(1)} %get-tuple-element.19.own_ref), channel_id=1, source_target_pairs={{0,1},{1,0},{2,3},{3,2},{4,5},{5,4},{6,7},{7,6},{8,9},{9,8},{10,11... | collective-permute-start | bytes 393224 | tf_op jit(solution)/shard_map/ppermute | solution.py:492
  8.5 15.1 %collective-permute-start.2 = (f32[2,4,8,512]{3,2,1,0:T(8,128)S(1)}, f32[2,4,8,512]{3,2,1,0:T(8,128)S(1)}, u32[]{:S(2)}, u32[]{:S(2)}) collective-permute-start(f32[2,4,8,512]{3,2,1,0:T(8,128)S(1)} %collective-permute-done.other_ref), channel_id=1, source_target_pairs={{0,8},{1,2},{2,1},{3,11},{4,12},{5,6},{6,5},{7,15},{8,0},{9,10},{1... | collective-permute-start | bytes 393224 | tf_op jit(solution)/shard_map/ppermute | solution.py:492
  8.5 15.1 %collective-permute-start.1 = (f32[2,4,8,512]{3,2,1,0:T(8,128)S(1)}, f32[2,4,8,512]{3,2,1,0:T(8,128)S(1)}, u32[]{:S(2)}, u32[]{:S(2)}) collective-permute-start(f32[2,4,8,512]{3,2,1,0:T(8,128)S(1)} %collective-permute-done.other_ref), channel_id=1, source_target_pairs={{0,1},{1,0},{2,3},{3,2},{4,5},{5,4},{6,7},{7,6},{8,9},{9,8},{10,11... | collective-permute-start | bytes 393224 | tf_op jit(solution)/shard_map/ppermute | solution.py:492
  11.9 4.5 %collective-permute-start.3 = (f32[3,128]{1,0:T(4,128)S(1)}, f32[3,128]{1,0:T(4,128)S(1)}, u32[]{:S(2)}, u32[]{:S(2)}) collective-permute-start(f32[3,128]{1,0:T(4,128)S(1)} %get-tuple-element.22), channel_id=1, source_target_pairs={{0,2},{1,3},{2,0},{3,1},{4,6},{5,7},{6,4},{7,5},{8,10},{9,11},{10,... | collective-permute-start | bytes 4616 | tf_op jit(solution)/shard_map/ppermute | solution.py:498
  16.3 3.6 %collective-permute-start.4 = (f32[3,128]{1,0:T(4,128)S(1)}, f32[3,128]{1,0:T(4,128)S(1)}, u32[]{:S(2)}, u32[]{:S(2)}) collective-permute-start(f32[3,128]{1,0:T(4,128)S(1)} %add.9), channel_id=1, source_target_pairs={{0,1},{1,0},{2,3},{3,2},{4,5},{5,4},{6,7},{7,6},{8,9},{9,8},{10,11... | collective-permute-start | bytes 4616 | tf_op jit(solution)/shard_map/ppermute | solution.py:498
  19.9 3.6 %collective-permute-start.5 = (f32[3,128]{1,0:T(4,128)S(1)}, f32[3,128]{1,0:T(4,128)S(1)}, u32[]{:S(2)}, u32[]{:S(2)}) collective-permute-start(f32[3,128]{1,0:T(4,128)S(1)} %add.10), channel_id=1, source_target_pairs={{0,4},{4,0},{1,5},{5,1},{2,6},{6,2},{3,7},{7,3},{8,12},{12,8},{9,1... | collective-permute-start | bytes 4616 | tf_op jit(solution)/shard_map/ppermute | solution.py:498
  25.7 13.4 %copy-start = (f32[64,4,8,128]{3,2,1,0:T(8,128)S(1)}, f32[64,4,8,128]{3,2,1,0:T(8,128)}, u32[]{:S(2)}) copy-start(f32[64,4,8,128]{3,2,1,0:T(8,128)} %phi_ref.3) | copy-start | bytes 3145732
  36.0 3.2 %copy-start.1 = (f32[32,4,8,128]{3,2,1,0:T(8,128)S(1)}, f32[32,4,8,128]{3,2,1,0:T(8,128)}, u32[]{:S(2)}) copy-start(f32[32,4,8,128]{3,2,1,0:T(8,128)} %psi_ref.3) | copy-start | bytes 1572868
  37.2 1.9 %collective-permute-start.8 = (f32[4,8,128]{2,1,0:T(8,128)S(1)}, f32[4,8,128]{2,1,0:T(8,128)S(1)}, u32[]{:S(2)}, u32[]{:S(2)}) collective-permute-start(f32[4,8,128]{2,1,0:T(8,128)S(1)} %get-tuple-element.30), channel_id=1, source_target_pairs={{0,8},{8,0},{16,24},{24,16},{1,9},{9,1},{17,25},{25,17},{2,10},{10... | collective-permute-start | bytes 49160 | tf_op jit(solution)/shard_map/ppermute | solution.py:520
  37.3 3.8 %collective-permute-start.9 = (f32[4,8,128]{2,1,0:T(8,128)S(1)}, f32[4,8,128]{2,1,0:T(8,128)S(1)}, u32[]{:S(2)}, u32[]{:S(2)}) collective-permute-start(f32[4,8,128]{2,1,0:T(8,128)S(1)} %get-tuple-element.31), channel_id=1, source_target_pairs={{0,16},{8,24},{16,0},{24,8},{1,17},{9,25},{17,1},{25,9},{2,18},{10... | collective-permute-start | bytes 49160 | tf_op jit(solution)/shard_map/ppermute | solution.py:520
  38.8 3.2 %collective-permute-start.10 = (f32[4,8,128]{2,1,0:T(8,128)S(1)}, f32[4,8,128]{2,1,0:T(8,128)S(1)}, u32[]{:S(2)}, u32[]{:S(2)}) collective-permute-start(f32[4,8,128]{2,1,0:T(8,128)S(1)} %get-tuple-element.32), channel_id=1, source_target_pairs={{0,24},{8,16},{16,8},{24,0},{1,25},{9,17},{17,9},{25,1},{2,26},{10... | collective-permute-start | bytes 49160 | tf_op jit(solution)/shard_map/ppermute | solution.py:520
  39.7 6.2 %copy-start.2 = (f32[32,4,8,128]{3,2,1,0:T(8,128)S(1)}, f32[32,4,8,128]{3,2,1,0:T(8,128)}, u32[]{:S(2)}) copy-start(f32[32,4,8,128]{3,2,1,0:T(8,128)} %range_ref.1) | copy-start | bytes 1572868
  43.2 2.7 %copy-start.4 = (f32[4,32]{1,0:T(4,128)S(1)}, f32[4,32]{1,0:T(4,128)}, u32[]{:S(2)}) copy-start(f32[4,32]{1,0:T(4,128)} %omega_ref.1) | copy-start | bytes 1540
  43.2 10.0 %all-to-all-start.1 = ((f32[32,4,128]{2,1,0:T(4,128)}), f32[32,4,128]{2,1,0:T(4,128)S(1)}, u32[]{:S(2)}, u32[]{:S(2)}) async-start(f32[32,4,128]{2,1,0:T(4,128)} %shard_map.126), calls=%async_computation.1 | async-start | bytes 131072 | tf_op jit(solution)/shard_map/all_to_all | solution.py:440
  45.9 7.3 %copy-start.3 = (f32[64,64]{1,0:T(8,128)S(1)}, f32[64,64]{1,0:T(8,128)}, u32[]{:S(2)}) copy-start(f32[64,64]{1,0:T(8,128)} %core_ref.1) | copy-start | bytes 49156
  45.9 7.2 %copy-start.5 = (f32[64,4]{0,1:T(4,128)S(1)}, f32[64,4]{0,1:T(4,128)}, u32[]{:S(2)}) copy-start(f32[64,4]{0,1:T(4,128)} %param.17) | copy-start | bytes 3076

commit v4 on v3

--- a/solution.py
+++ b/solution.py
@@ -272,6 +272,8 @@
         (even_other_ref, rows_x, even_row, jacobi_weight),
         (odd_other_ref, rows_x, odd_row, odd_inside),
     )
+    weight_ref[...] = weight_from[...]
+    drive_ref[...] = drive_from[...]
     fill(blocks, weight_ref, drive_ref)
 
     parts = inverse_ref.shape[0] // LANES
@@ -417,7 +419,7 @@
 smem = pl.BlockSpec(memory_space=pltpu.SMEM)
 
 
-def call(kernel, outs, inputs, scratch=(), specs=None, aliases=None):
+def call(kernel, outs, inputs, scratch=(), specs=None):
     many = isinstance(outs, list)
     shapes = [jax.ShapeDtypeStruct(shape, jnp.float32) for shape in (outs if many else [outs])]
     result = pl.pallas_call(
@@ -427,7 +429,6 @@
         out_specs=[vmem] * len(shapes),
         scratch_shapes=[pltpu.VMEM(shape, jnp.float32) for shape in scratch],
         compiler_params=pltpu.CompilerParams(vmem_limit_bytes=VMEM_BYTES),
-        input_output_aliases=aliases or {},
     )(*inputs)
     return result if many else result[0]
 
@@ -506,7 +507,6 @@
         [padded, window, window, copies],
         (mine, others[2], others[4], ids, inverse, gathered, *prepared),
         scratch=[padded],
-        aliases={6: 1, 7: 2},
     )
     gathered = gather(partial, ("gx", "gy"))
     chunk = cells_z // groups

time: 54.3 us -> 54.4 us (level)
  no operation moved by 1% of the time
where the time goes in v4:
time: 54.4 us; the launch traced here: 54.1 us
  starting transfers between devices  17.5 us (32%)
  waiting for transfers between devices  16.8 us (31%)
  blocking collectives  10.2 us (19%)
  Pallas kernels  8.93 us (16%)
  between operations  0.75 us (1%)
    all_to_all x1, blocking collectives, gather(): return lax.all_to_all(copies, axes, 0, 0)  10.2 us
    ppermute x5, starting transfers between devices, fast_body(): others.append(lax.ppermute(sent, ('grp', 'gx', 'gy'), pairs(phase)))  9.58 us
    ppermute x3, waiting for transfers between devices, fast_body(): lax.ppermute(gathered, axis, [(i, i ^ bit) for i in range(count)])  8.37 us
    pallas_call x7, Pallas kernels, call(): pl.pallas_call(kernel, out_shape=shapes, in_specs=specs or [vmem] * len(i...  7.64 us
    all_to_all x1, waiting for transfers between devices, gather(): return lax.all_to_all(copies, axes, 0, 0)  5.7 us
    ppermute x3, starting transfers between devices, fast_body(): lax.ppermute(gathered, axis, [(i, i ^ bit) for i in range(count)])  3.28 us
    all_to_all x1, starting transfers between devices, gather(): return lax.all_to_all(copies, axes, 0, 0)  2.68 us
    ppermute x3, waiting for transfers between devices, fast_body(): lax.ppermute(pieces[turn], 'grp', [(at, at ^ turn) for at in range(groups)])  2.33 us
  transfers between devices with their start and end apart: 12, of which 7 were waited for; matrix products, arithmetic and copies ran while one was open for 0% of the time, Pallas kernels for 4%

profile of v4, /device:TPU:0, one launch (start us, length us, event | category | flops | bytes accessed | tf_op | source)
XLA Modules:
  0.0 54.1 jit_solution(8593040319491988856)
XLA Ops:
  0.6 1.3 %begin.1 = (f32[2,4,8,512]{3,2,1,0:T(8,128)S(1)}, s32[4,8,512]{2,1,0:T(8,128)S(1)}, f32[256,256]{1,0:T(8,128)S(1)}, f32[3,128]{1,0:T(4,128)S(1)}) custom-call(f32[4,8,512]{2,1,0:T(8,128)} %bitcast.4, f32[4,8,512]{2,1,0:T(8,128)} %diagonal_from.1, s32[4,8,512]{2,1,0:T(8,128)} %ids_from.1, f32[256,256]{1,0:T(8,128)} %inverse_from.1), custom_call_target="tpu_custom_call" | custom-call | tf_op jit(solution)/shard_map/begin/pallas_call | solution.py:476
  1.9 3.1 %collective-permute-start = (f32[2,4,8,512]{3,2,1,0:T(8,128)S(1)}, f32[2,4,8,512]{3,2,1,0:T(8,128)S(1)}, u32[]{:S(2)}, u32[]{:S(2)}) collective-permute-start(f32[2,4,8,512]{3,2,1,0:T(8,128)S(1)} %get-tuple-element.19.own_ref), channel_id=1, source_target_pairs={{0,4},{1,5},{2,6},{3,7},{4,0},{5,1},{6,2},{7,3},{8,12},{9,13},{10,... | collective-permute-start | bytes 393224 | tf_op jit(solution)/shard_map/ppermute | solution.py:493
  5.0 0.0 collective-permute-start.7
  5.0 3.1 %collective-permute-start.6 = (f32[2,4,8,512]{3,2,1,0:T(8,128)S(1)}, f32[2,4,8,512]{3,2,1,0:T(8,128)S(1)}, u32[]{:S(2)}, u32[]{:S(2)}) collective-permute-start(f32[2,4,8,512]{3,2,1,0:T(8,128)S(1)} %get-tuple-element.19.own_ref), channel_id=1, source_target_pairs={{0,1},{1,0},{2,3},{3,2},{4,5},{5,4},{6,7},{7,6},{8,9},{9,8},{10,11... | collective-permute-start | bytes 393224 | tf_op jit(solution)/shard_map/ppermute | solution.py:493
  8.1 0.3 collective-permute-done.other_ref
  8.5 0.0 collective-permute-start.2
  8.5 3.4 %collective-permute-start.1 = (f32[2,4,8,512]{3,2,1,0:T(8,128)S(1)}, f32[2,4,8,512]{3,2,1,0:T(8,128)S(1)}, u32[]{:S(2)}, u32[]{:S(2)}) collective-permute-start(f32[2,4,8,512]{3,2,1,0:T(8,128)S(1)} %collective-permute-done.other_ref), channel_id=1, source_target_pairs={{0,1},{1,0},{2,3},{3,2},{4,5},{5,4},{6,7},{7,6},{8,9},{9,8},{10,11... | collective-permute-start | bytes 393224 | tf_op jit(solution)/shard_map/ppermute | solution.py:493
  11.9 1.0 %collective-permute-start.3 = (f32[3,128]{1,0:T(4,128)S(1)}, f32[3,128]{1,0:T(4,128)S(1)}, u32[]{:S(2)}, u32[]{:S(2)}) collective-permute-start(f32[3,128]{1,0:T(4,128)S(1)} %get-tuple-element.22), channel_id=1, source_target_pairs={{0,2},{1,3},{2,0},{3,1},{4,6},{5,7},{6,4},{7,5},{8,10},{9,11},{10,... | collective-permute-start | bytes 4616 | tf_op jit(solution)/shard_map/ppermute | solution.py:499
  12.9 3.5 %collective-permute-done.3 = f32[3,128]{1,0:T(4,128)S(1)} collective-permute-done((f32[3,128]{1,0:T(4,128)S(1)}, f32[3,128]{1,0:T(4,128)S(1)}, u32[]{:S(2)}, u32[]{:S(2)}) %collective-permute-start.3) | collective-permute-done | bytes 1568 | tf_op jit(solution)/shard_map/ppermute | solution.py:499
  16.3 0.7 %collective-permute-start.4 = (f32[3,128]{1,0:T(4,128)S(1)}, f32[3,128]{1,0:T(4,128)S(1)}, u32[]{:S(2)}, u32[]{:S(2)}) collective-permute-start(f32[3,128]{1,0:T(4,128)S(1)} %add.9), channel_id=1, source_target_pairs={{0,1},{1,0},{2,3},{3,2},{4,5},{5,4},{6,7},{7,6},{8,9},{9,8},{10,11... | collective-permute-start | bytes 4616 | tf_op jit(solution)/shard_map/ppermute | solution.py:499
  17.1 2.8 %collective-permute-done.4 = f32[3,128]{1,0:T(4,128)S(1)} collective-permute-done((f32[3,128]{1,0:T(4,128)S(1)}, f32[3,128]{1,0:T(4,128)S(1)}, u32[]{:S(2)}, u32[]{:S(2)}) %collective-permute-start.4) | collective-permute-done | bytes 1568 | tf_op jit(solution)/shard_map/ppermute | solution.py:499
  19.9 1.5 %collective-permute-start.5 = (f32[3,128]{1,0:T(4,128)S(1)}, f32[3,128]{1,0:T(4,128)S(1)}, u32[]{:S(2)}, u32[]{:S(2)}) collective-permute-start(f32[3,128]{1,0:T(4,128)S(1)} %add.10), channel_id=1, source_target_pairs={{0,4},{4,0},{1,5},{5,1},{2,6},{6,2},{3,7},{7,3},{8,12},{12,8},{9,1... | collective-permute-start | bytes 4616 | tf_op jit(solution)/shard_map/ppermute | solution.py:499
  21.5 2.1 %collective-permute-done.5 = f32[3,128]{1,0:T(4,128)S(1)} collective-permute-done((f32[3,128]{1,0:T(4,128)S(1)}, f32[3,128]{1,0:T(4,128)S(1)}, u32[]{:S(2)}, u32[]{:S(2)}) %collective-permute-start.5) | collective-permute-done | bytes 1568 | tf_op jit(solution)/shard_map/ppermute | solution.py:499
  23.5 0.0 collective-permute-done.7.odd_ref
  23.5 0.0 collective-permute-done.6.even_ref
  23.5 0.1 shard_map.121
  23.6 0.0 collective-permute-done.2.odd_other_ref
  23.6 0.0 collective-permute-done.1.even_other_ref
  23.6 2.2 %shard_map.122 = (f32[10,24,512]{2,1,0:T(8,128)S(1)}, f32[8,24,512]{2,1,0:T(8,128)S(1)}, f32[8,24,512]{2,1,0:T(8,128)S(1)}, f32[8,3,128]{2,1,0:T(4,128)S(1)}) custom-call(f32[2,4,8,512]{3,2,1,0:T(8,128)S(1)} %get-tuple-element.19.own_ref, f32[2,4,8,512]{3,2,1,0:T(8,128)S(1)} %collective-permute-done.1.even_other_ref, ...), custom_call_target="tpu_custom_call" | custom-call | tf_op jit(solution)/shard_map/pallas_call | solution.py:425
  25.8 0.0 copy-start
  25.8 10.2 %all_to_all.10.gathered_ref = f32[8,3,128]{2,1,0:T(4,128)S(1)} all-to-all(f32[8,3,128]{2,1,0:T(4,128)S(1)} %get-tuple-element.28), channel_id=1, replica_groups=mesh['grp'=4,'gx'=2,'gy'=4] {'gx','gy'}, dimensions={0} | all-to-all | bytes 24576 | tf_op jit(solution)/shard_map/all_to_all | solution.py:441
  36.0 0.0 copy-start.1
  36.0 1.2 %shard_map.123 = (f32[4,8,128]{2,1,0:T(8,128)S(1)}, f32[4,8,128]{2,1,0:T(8,128)S(1)}, f32[4,8,128]{2,1,0:T(8,128)S(1)}, f32[4,8,128]{2,1,0:T(8,128)S(1)}) custom-call(f32[10,24,512]{2,1,0:T(8,128)S(1)} %get-tuple-element.25.field_ref, f32[8,24,512]{2,1,0:T(8,128)S(1)} %get-tuple-element.26.weight_ref, f32[8,24,512]{2,1,0:T(8,128)S(1)} %get-tuple-element.27.drive_ref, ...), custom_call_target="tpu_custom_call" | custom-call | tf_op jit(solution)/shard_map/pallas_call | solution.py:425
  37.2 0.1 collective-permute-start.8
  37.3 1.6 %collective-permute-start.9 = (f32[4,8,128]{2,1,0:T(8,128)S(1)}, f32[4,8,128]{2,1,0:T(8,128)S(1)}, u32[]{:S(2)}, u32[]{:S(2)}) collective-permute-start(f32[4,8,128]{2,1,0:T(8,128)S(1)} %get-tuple-element.31), channel_id=1, source_target_pairs={{0,16},{8,24},{16,0},{24,8},{1,17},{9,25},{17,1},{25,9},{2,18},{10... | collective-permute-start | bytes 49160 | tf_op jit(solution)/shard_map/ppermute | solution.py:520
  38.9 0.3 collective-permute-start.10
  39.2 0.0 collective-permute-done.8.rest_1_
  39.2 0.0 copy-done
  39.2 0.0 copy-done.1
  39.2 0.5 shard_map.125.early_ref
  39.7 0.0 copy-start.2
  39.7 1.4 %collective-permute-done.9.rest_2_.rest_0_ = f32[4,8,128]{2,1,0:T(8,128)S(1)} collective-permute-done((f32[4,8,128]{2,1,0:T(8,128)S(1)}, f32[4,8,128]{2,1,0:T(8,128)S(1)}, u32[]{:S(2)}, u32[]{:S(2)}) %collective-permute-start.9) | collective-permute-done | bytes 16416 | tf_op jit(solution)/shard_map/ppermute | solution.py:520
  41.1 0.9 %collective-permute-done.10.rest_3_.rest_1_ = f32[4,8,128]{2,1,0:T(8,128)S(1)} collective-permute-done((f32[4,8,128]{2,1,0:T(8,128)S(1)}, f32[4,8,128]{2,1,0:T(8,128)S(1)}, u32[]{:S(2)}, u32[]{:S(2)}) %collective-permute-start.10) | collective-permute-done | bytes 16416 | tf_op jit(solution)/shard_map/ppermute | solution.py:520
  42.0 1.2 %shard_map.126 = f32[32,4,128]{2,1,0:T(4,128)} custom-call(f32[32,4,8,128]{3,2,1,0:T(8,128)S(1)} %copy-done.1, f32[64,4,8,128]{3,2,1,0:T(8,128)S(1)} %copy-done, f32[2,128]{1,0:T(2,128)S(1)} %shard_map.125.early_ref, f32[4,8,128]{2,1,0:T(8,128)S(1)} %collective-permute-done.9.rest_2_.rest_0_, f32[4,8,128]{2,1,0:T(8,128)S(1)} %collective-permute-done.10.rest_3_.rest_1_), custom_call_target="tpu_custom_call" | custom-call | tf_op jit(solution)/shard_map/pallas_call | solution.py:425
  43.2 0.0 copy-start.4
  43.2 2.7 %all-to-all-start.1 = ((f32[32,4,128]{2,1,0:T(4,128)}), f32[32,4,128]{2,1,0:T(4,128)S(1)}, u32[]{:S(2)}, u32[]{:S(2)}) async-start(f32[32,4,128]{2,1,0:T(4,128)} %shard_map.126), calls=%async_computation.1 | async-start | bytes 131072 | tf_op jit(solution)/shard_map/all_to_all | solution.py:441
  45.9 0.0 copy-done.2
  45.9 0.0 copy-done.4
  45.9 0.0 copy-start.3
  45.9 0.0 copy-start.5
  46.0 1.5 %shard_map.124 = f32[32,4,8,128]{3,2,1,0:T(8,128)} custom-call(f32[4,32]{1,0:T(4,128)S(1)} %copy-done.4, f32[32,4,8,128]{3,2,1,0:T(8,128)S(1)} %copy-done.2, f32[4,8,128]{2,1,0:T(8,128)S(1)} %get-tuple-element.29.rest_0_, f32[4,8,128]{2,1,0:T(8,128)S(1)} %collective-permute-done.8.rest_1_, f32[4,8,128]{2,1,0:T(8,128)S(1)} %collective-permute-done.9.rest_2_.rest_0_, ...), custom_call_target="tpu_custom_call" | custom-call | tf_op jit(solution)/shard_map/pallas_call | solution.py:425
  47.5 5.7 %all-to-all-done.1.gathered_ref = f32[32,4,128]{2,1,0:T(4,128)S(1)} async-done(((f32[32,4,128]{2,1,0:T(4,128)}), f32[32,4,128]{2,1,0:T(4,128)S(1)}, u32[]{:S(2)}, u32[]{:S(2)}) %all-to-all-start.1) | async-done | bytes 65568 | tf_op jit(solution)/shard_map/all_to_all | solution.py:441
  53.2 0.0 copy-done.3
  53.2 0.0 copy-done.5
  53.2 0.9 %shard_map.127 = (f32[4,32]{1,0:T(4,128)}, f32[64,64]{1,0:T(8,128)}) custom-call(f32[32,4,128]{2,1,0:T(4,128)S(1)} %all-to-all-done.1.gathered_ref, f32[4,64]{1,0:T(4,128)S(1)} %bitcast.3, f32[64,64]{1,0:T(8,128)S(1)} %copy-done.3), custom_call_target="tpu_custom_call" | custom-call | tf_op jit(solution)/shard_map/pallas_call | solution.py:425
  (3 shorter events, 0.0 us)
Async XLA Ops:
  1.9 6.6 %collective-permute-start = (f32[2,4,8,512]{3,2,1,0:T(8,128)S(1)}, f32[2,4,8,512]{3,2,1,0:T(8,128)S(1)}, u32[]{:S(2)}, u32[]{:S(2)}) collective-permute-start(f32[2,4,8,512]{3,2,1,0:T(8,128)S(1)} %get-tuple-element.19.own_ref), channel_id=1, source_target_pairs={{0,4},{1,5},{2,6},{3,7},{4,0},{5,1},{6,2},{7,3},{8,12},{9,13},{10,... | collective-permute-start | bytes 393224 | tf_op jit(solution)/shard_map/ppermute | solution.py:493
  5.0 18.5 %collective-permute-start.7 = (f32[2,4,8,512]{3,2,1,0:T(8,128)S(1)}, f32[2,4,8,512]{3,2,1,0:T(8,128)S(1)}, u32[]{:S(2)}, u32[]{:S(2)}) collective-permute-start(f32[2,4,8,512]{3,2,1,0:T(8,128)S(1)} %get-tuple-element.19.own_ref), channel_id=1, source_target_pairs={{0,8},{1,2},{2,1},{3,11},{4,12},{5,6},{6,5},{7,15},{8,0},{9,10},{1... | collective-permute-start | bytes 393224 | tf_op jit(solution)/shard_map/ppermute | solution.py:493
  5.0 18.5 %collective-permute-start.6 = (f32[2,4,8,512]{3,2,1,0:T(8,128)S(1)}, f32[2,4,8,512]{3,2,1,0:T(8,128)S(1)}, u32[]{:S(2)}, u32[]{:S(2)}) collective-permute-start(f32[2,4,8,512]{3,2,1,0:T(8,128)S(1)} %get-tuple-element.19.own_ref), channel_id=1, source_target_pairs={{0,1},{1,0},{2,3},{3,2},{4,5},{5,4},{6,7},{7,6},{8,9},{9,8},{10,11... | collective-permute-start | bytes 393224 | tf_op jit(solution)/shard_map/ppermute | solution.py:493
  8.5 15.1 %collective-permute-start.2 = (f32[2,4,8,512]{3,2,1,0:T(8,128)S(1)}, f32[2,4,8,512]{3,2,1,0:T(8,128)S(1)}, u32[]{:S(2)}, u32[]{:S(2)}) collective-permute-start(f32[2,4,8,512]{3,2,1,0:T(8,128)S(1)} %collective-permute-done.other_ref), channel_id=1, source_target_pairs={{0,8},{1,2},{2,1},{3,11},{4,12},{5,6},{6,5},{7,15},{8,0},{9,10},{1... | collective-permute-start | bytes 393224 | tf_op jit(solution)/shard_map/ppermute | solution.py:493
  8.5 15.1 %collective-permute-start.1 = (f32[2,4,8,512]{3,2,1,0:T(8,128)S(1)}, f32[2,4,8,512]{3,2,1,0:T(8,128)S(1)}, u32[]{:S(2)}, u32[]{:S(2)}) collective-permute-start(f32[2,4,8,512]{3,2,1,0:T(8,128)S(1)} %collective-permute-done.other_ref), channel_id=1, source_target_pairs={{0,1},{1,0},{2,3},{3,2},{4,5},{5,4},{6,7},{7,6},{8,9},{9,8},{10,11... | collective-permute-start | bytes 393224 | tf_op jit(solution)/shard_map/ppermute | solution.py:493
  11.9 4.5 %collective-permute-start.3 = (f32[3,128]{1,0:T(4,128)S(1)}, f32[3,128]{1,0:T(4,128)S(1)}, u32[]{:S(2)}, u32[]{:S(2)}) collective-permute-start(f32[3,128]{1,0:T(4,128)S(1)} %get-tuple-element.22), channel_id=1, source_target_pairs={{0,2},{1,3},{2,0},{3,1},{4,6},{5,7},{6,4},{7,5},{8,10},{9,11},{10,... | collective-permute-start | bytes 4616 | tf_op jit(solution)/shard_map/ppermute | solution.py:499
  16.3 3.6 %collective-permute-start.4 = (f32[3,128]{1,0:T(4,128)S(1)}, f32[3,128]{1,0:T(4,128)S(1)}, u32[]{:S(2)}, u32[]{:S(2)}) collective-permute-start(f32[3,128]{1,0:T(4,128)S(1)} %add.9), channel_id=1, source_target_pairs={{0,1},{1,0},{2,3},{3,2},{4,5},{5,4},{6,7},{7,6},{8,9},{9,8},{10,11... | collective-permute-start | bytes 4616 | tf_op jit(solution)/shard_map/ppermute | solution.py:499
  19.9 3.6 %collective-permute-start.5 = (f32[3,128]{1,0:T(4,128)S(1)}, f32[3,128]{1,0:T(4,128)S(1)}, u32[]{:S(2)}, u32[]{:S(2)}) collective-permute-start(f32[3,128]{1,0:T(4,128)S(1)} %add.10), channel_id=1, source_target_pairs={{0,4},{4,0},{1,5},{5,1},{2,6},{6,2},{3,7},{7,3},{8,12},{12,8},{9,1... | collective-permute-start | bytes 4616 | tf_op jit(solution)/shard_map/ppermute | solution.py:499
  25.8 13.4 %copy-start = (f32[64,4,8,128]{3,2,1,0:T(8,128)S(1)}, f32[64,4,8,128]{3,2,1,0:T(8,128)}, u32[]{:S(2)}) copy-start(f32[64,4,8,128]{3,2,1,0:T(8,128)} %phi_ref.3) | copy-start | bytes 3145732
  36.0 3.2 %copy-start.1 = (f32[32,4,8,128]{3,2,1,0:T(8,128)S(1)}, f32[32,4,8,128]{3,2,1,0:T(8,128)}, u32[]{:S(2)}) copy-start(f32[32,4,8,128]{3,2,1,0:T(8,128)} %psi_ref.3) | copy-start | bytes 1572868
  37.2 1.9 %collective-permute-start.8 = (f32[4,8,128]{2,1,0:T(8,128)S(1)}, f32[4,8,128]{2,1,0:T(8,128)S(1)}, u32[]{:S(2)}, u32[]{:S(2)}) collective-permute-start(f32[4,8,128]{2,1,0:T(8,128)S(1)} %get-tuple-element.30), channel_id=1, source_target_pairs={{0,8},{8,0},{16,24},{24,16},{1,9},{9,1},{17,25},{25,17},{2,10},{10... | collective-permute-start | bytes 49160 | tf_op jit(solution)/shard_map/ppermute | solution.py:520
  37.3 3.8 %collective-permute-start.9 = (f32[4,8,128]{2,1,0:T(8,128)S(1)}, f32[4,8,128]{2,1,0:T(8,128)S(1)}, u32[]{:S(2)}, u32[]{:S(2)}) collective-permute-start(f32[4,8,128]{2,1,0:T(8,128)S(1)} %get-tuple-element.31), channel_id=1, source_target_pairs={{0,16},{8,24},{16,0},{24,8},{1,17},{9,25},{17,1},{25,9},{2,18},{10... | collective-permute-start | bytes 49160 | tf_op jit(solution)/shard_map/ppermute | solution.py:520
  38.9 3.2 %collective-permute-start.10 = (f32[4,8,128]{2,1,0:T(8,128)S(1)}, f32[4,8,128]{2,1,0:T(8,128)S(1)}, u32[]{:S(2)}, u32[]{:S(2)}) collective-permute-start(f32[4,8,128]{2,1,0:T(8,128)S(1)} %get-tuple-element.32), channel_id=1, source_target_pairs={{0,24},{8,16},{16,8},{24,0},{1,25},{9,17},{17,9},{25,1},{2,26},{10... | collective-permute-start | bytes 49160 | tf_op jit(solution)/shard_map/ppermute | solution.py:520
  39.7 6.2 %copy-start.2 = (f32[32,4,8,128]{3,2,1,0:T(8,128)S(1)}, f32[32,4,8,128]{3,2,1,0:T(8,128)}, u32[]{:S(2)}) copy-start(f32[32,4,8,128]{3,2,1,0:T(8,128)} %range_ref.1) | copy-start | bytes 1572868
  43.2 2.7 %copy-start.4 = (f32[4,32]{1,0:T(4,128)S(1)}, f32[4,32]{1,0:T(4,128)}, u32[]{:S(2)}) copy-start(f32[4,32]{1,0:T(4,128)} %omega_ref.1) | copy-start | bytes 1540
  43.2 10.0 %all-to-all-start.1 = ((f32[32,4,128]{2,1,0:T(4,128)}), f32[32,4,128]{2,1,0:T(4,128)S(1)}, u32[]{:S(2)}, u32[]{:S(2)}) async-start(f32[32,4,128]{2,1,0:T(4,128)} %shard_map.126), calls=%async_computation.1 | async-start | bytes 131072 | tf_op jit(solution)/shard_map/all_to_all | solution.py:441
  45.9 7.3 %copy-start.3 = (f32[64,64]{1,0:T(8,128)S(1)}, f32[64,64]{1,0:T(8,128)}, u32[]{:S(2)}) copy-start(f32[64,64]{1,0:T(8,128)} %core_ref.1) | copy-start | bytes 49156
  45.9 7.2 %copy-start.5 = (f32[64,4]{0,1:T(4,128)S(1)}, f32[64,4]{0,1:T(4,128)}, u32[]{:S(2)}) copy-start(f32[64,4]{0,1:T(4,128)} %param.17) | copy-start | bytes 3076
